TPU v7x, 256 devices: a whole 4x4x8 slice. The times are simulated.
256 devices in a mesh: dp: 4 (over y), ctx: 64 (over z, x, core).
Axes of the slice: x: 4, y: 4, z: 8, core: 2. Of those that a mesh axis runs over, the one named last changes fastest.
Arguments:
- gate_in: bfloat16 [4, 8192, 2048], P('dp', 'ctx'), may hold values from -6 to 6
- key_in: bfloat16 [4, 8192, 2048], P('dp', 'ctx'), may hold values from -6 to 6
- value_in: bfloat16 [4, 8192, 2048], P('dp', 'ctx'), may hold values from -6 to 6
- cotangent: bfloat16 [4, 8192, 2048], P('dp', 'ctx'), may hold values from -6 to 6
- doc_starts: int32 [4, 17], P('dp'), may hold values from 0 to 7936, as said below
- filters: bfloat16 [128, 128], replicated, may hold values from -0.5 to 0.5
Outputs:
- output: bfloat16 [4, 8192, 2048], P('dp', 'ctx')
- grad_query: bfloat16 [4, 8192, 2048], P('dp', 'ctx')
- grad_key: bfloat16 [4, 8192, 2048], P('dp', 'ctx')
- grad_value: bfloat16 [4, 8192, 2048], P('dp', 'ctx')
- filter_grad: float32 [128, 128], replicated
Inputs may be any that keep to these rules, and one draw needn't show every extreme that they name: `doc_starts`: each row holds 17 strictly rising multiples of 128; the first is 0 and the last is 7936.
All inputs are finite; a program needn't handle non-finite values.
Results may differ from a plain program's by a relative error of at most 0.0049.
Values may be sent and summed in bfloat16 or wider, within the bound.
A program may use at most 192 MiB of HBM per device.

v0:
```python
import jax
import jax.numpy as jnp
from jax import lax
from jax.sharding import PartitionSpec as P


def shifted(array, axis, by):
    size = lax.axis_size(axis)
    pairs = [(i, i + by) for i in range(size) if 0 <= i + by < size]
    return lax.ppermute(array, axis, pairs)


def split_up(array, dim, size):
    before, after = (array.shape[:dim], array.shape[dim + 1 :])
    return jnp.moveaxis(array.reshape(*before, size, -1, *after), dim, 0)


def summed_on_arrival(array, axis, dim):
    tiles = split_up(array, dim, lax.axis_size(axis))
    arrived = lax.all_to_all(tiles, axis, split_axis=0, concat_axis=0, tiled=True)
    return arrived.sum(axis=0)


def rows_for(lines, size):
    spare = -len(lines) % size
    return jnp.pad(lines, [(0, spare)] + [(0, 0)] * (lines.ndim - 1))


def in_order(tiles, dim):
    tiles = jnp.moveaxis(tiles, 0, dim)
    lengths = tiles.shape
    return tiles.reshape(*lengths[:dim], lengths[dim] * lengths[dim + 1], *lengths[dim + 2 :])


def from_everyone(array, axis):
    copies = jnp.broadcast_to(array, (lax.axis_size(axis), *array.shape))
    return lax.all_to_all(copies, axis, split_axis=0, concat_axis=0, tiled=True)


def gather_directly(array, axis, dim):
    return in_order(from_everyone(array, axis), dim)


def total_of(array, axes):
    lines = array.reshape(-1, array.shape[-1])
    own = summed_on_arrival(rows_for(lines, lax.axis_size(axes)), axes, 0)
    whole = gather_directly(own, axes, 0)
    return whole[: len(lines)].reshape(array.shape)


def of_everyone(array, axis):
    return from_everyone(array, axis).sum(axis=0)


def build_tiles(filters):
    group_count = filters.shape[0]
    tap_count = filters.shape[1]
    zero_block = jnp.zeros((group_count, tap_count), filters.dtype)
    diag_line = jnp.concatenate([zero_block, filters[:, ::-1], zero_block], axis=1)
    flattened = jnp.tile(diag_line, (1, tap_count))
    stride = 3 * tap_count - 1
    flattened = flattened[:, tap_count - 1 : tap_count - 1 + tap_count * stride]
    return flattened.reshape(group_count, tap_count, stride)[:, :, : 2 * tap_count]


def diagonal_sums(tile_grads):
    group_count = tile_grads.shape[0]
    tap_count = tile_grads.shape[1]
    stride = 3 * tap_count - 1
    padded = jnp.pad(tile_grads, ((0, 0), (0, 0), (0, stride - 2 * tap_count)))
    flattened = padded.reshape(group_count, tap_count * stride)
    flattened = jnp.pad(flattened, ((0, 0), (tap_count - 1, 1)))
    diag_line = jnp.sum(flattened.reshape(group_count, tap_count, 3 * tap_count), axis=1)
    return diag_line[:, tap_count : 2 * tap_count][:, ::-1]


def keep_mask(starts_row, first_block, block_total, tap_count):
    block_ids = first_block + jnp.arange(block_total, dtype=jnp.int32)
    is_start = jnp.any(starts_row[None, :] == block_ids[:, None] * tap_count, axis=1)
    return jnp.where(is_start, 0.0, 1.0).astype(jnp.float32)


def per_device(gate_in, key_in, value_in, cotangent, doc_starts, filters):
    row_count = gate_in.shape[1]
    channels = gate_in.shape[2]
    tap_count = filters.shape[1]
    group_count = filters.shape[0]
    group_width = channels // group_count
    block_count = row_count // tap_count
    gate_local = gate_in[0]
    key_local = key_in[0]
    value_local = value_in[0]
    upstream = cotangent[0]
    first_block = lax.axis_index("ctx") * block_count
    keep_vals = keep_mask(doc_starts[0], first_block, block_count + 1, tap_count)
    product = (key_local.astype(jnp.float32) * value_local.astype(jnp.float32)).astype(jnp.bfloat16)
    before = shifted(product, "ctx", 1)
    shaped = product.reshape(block_count, tap_count, group_count, group_width)
    earlier = jnp.concatenate(
        [before.reshape(1, tap_count, group_count, group_width), shaped[:-1]], axis=0
    )
    earlier = earlier * keep_vals[:block_count, None, None, None].astype(jnp.bfloat16)
    window = jnp.concatenate([earlier, shaped], axis=1)
    toeplitz = build_tiles(filters)
    conv_out = jnp.einsum("ftj,bjfc->btfc", toeplitz, window, preferred_element_type=jnp.float32)
    conv_out = conv_out.reshape(row_count, channels)
    output = (gate_local.astype(jnp.float32) * conv_out).astype(jnp.bfloat16)
    grad_query = (upstream.astype(jnp.float32) * conv_out).astype(jnp.bfloat16)
    grad_conv = (upstream.astype(jnp.float32) * gate_local.astype(jnp.float32)).astype(jnp.bfloat16)
    grad_blocks = grad_conv.reshape(block_count, tap_count, group_count, group_width)
    spread = jnp.einsum("ftj,btfc->bjfc", toeplitz, grad_blocks, preferred_element_type=jnp.float32)
    current = spread[:, tap_count:]
    carried = spread[:, :tap_count] * keep_vals[:block_count, None, None, None]
    incoming = shifted(carried[0].reshape(tap_count, channels), "ctx", -1)
    incoming = incoming.reshape(tap_count, group_count, group_width)
    following = jnp.concatenate([carried[1:], incoming[None]], axis=0)
    grad_mixed = (current + following).reshape(row_count, channels)
    grad_key = (grad_mixed * value_local.astype(jnp.float32)).astype(jnp.bfloat16)
    grad_value = (grad_mixed * key_local.astype(jnp.float32)).astype(jnp.bfloat16)
    tile_grads = jnp.einsum(
        "btfc,bjfc->ftj", grad_blocks, window, preferred_element_type=jnp.float32
    )
    local_terms = diagonal_sums(tile_grads)
    sequence_terms = total_of(local_terms, "ctx")
    filter_grad = of_everyone(sequence_terms, "dp")
    return (output[None], grad_query[None], grad_key[None], grad_value[None], filter_grad)


def solution(mesh):
    placed = (
        P("dp", "ctx", None),
        P("dp", "ctx", None),
        P("dp", "ctx", None),
        P("dp", "ctx", None),
        P("dp", None),
        P(),
    )
    return jax.shard_map(
        per_device,
        mesh=mesh,
        in_specs=placed,
        out_specs=(
            P("dp", "ctx", None),
            P("dp", "ctx", None),
            P("dp", "ctx", None),
            P("dp", "ctx", None),
            P(),
        ),
        check_vma=False,
    )
```

profile of v0, /device:TPU:1, one launch (start us, length us, event | category | flops | bytes accessed | tf_op | source)
XLA Modules:
  0.0 217.8 jit_solution(11816613231719583722)
XLA Ops:
  0.6 0.8 compare_reduce_fusion
  1.5 0.8 rev.6
  2.3 1.3 copy.35
  3.7 1.3 copy.38
  5.0 5.7 %tile.4 = bf16[128,128,384]{2,1,0:T(8,128)(2,1)} broadcast(bf16[128,384]{1,0:T(8,128)(2,1)S(1)} %pad_maximum_fusion), dimensions={0,2} | broadcast | bytes 12681216 | tf_op jit(solution)/shard_map/tile | solution.py:60
  10.7 12.5 %copy.45 = bf16[16,8,128,384]{3,1,2,0:T(8,128)(2,1)S(1)} copy(bf16[16,8,128,384]{3,2,1,0:T(8,128)(2,1)} %bitcast.36) | data formatting | bytes 25165824
  23.2 6.6 %slice.25 = bf16[128,49024]{1,0:T(8,128)(2,1)} slice(bf16[128,49152]{1,0:T(8,128)(2,1)S(1)} %bitcast.37), slice={[0:128], [127:49151]} | slice | bytes 25100288 | tf_op jit(solution)/shard_map/slice | solution.py:62
  29.8 30.8 %reshape.122 = bf16[128,128,383]{2,1,0:T(8,128)(2,1)} reshape(bf16[128,49024]{1,0:T(8,128)(2,1)} %slice.25) | data formatting | bytes 25100288 | tf_op jit(solution)/shard_map/reshape | solution.py:63
  60.6 0.1 fusion.12
  60.8 4.6 %fusion.4 = f32[1,256,128,16]{1,3,2,0:T(8,128)S(1)} fusion(bf16[128,128,16]{0,2,1:T(8,128)(2,1)S(1)} %bitcast.42, bf16[128,128,383]{2,1,0:T(8,128)(2,1)} %reshape.122), kind=kOutput, calls=%fused_computation.5 | convolution fusion | flops 134217728 | bytes 11010048 | tf_op jit(solution)/shard_map/ftj,btfc->bjfc/dot_general | solution.py:111
  65.4 0.2 slice_multiply_fusion
  65.6 5.1 %collective-permute-start.1 = (f32[128,2048]{0,1:T(8,128)S(1)}, f32[128,2048]{0,1:T(8,128)S(1)}, u32[]{:S(2)}, u32[]{:S(2)}) collective-permute-start(f32[128,2048]{0,1:T(8,128)S(1)} %bitcast.47), channel_id=1, source_target_pairs={{1,0},{2,1},{3,2},{4,3},{5,4},{6,5},{7,6},{8,7},{9,8},{10,9},{11,1... | collective-permute-start | bytes 3145736 | tf_op jit(solution)/shard_map/ppermute | solution.py:10
  70.7 11.9 %collective-permute-done.1 = f32[128,2048]{0,1:T(8,128)S(1)} collective-permute-done((f32[128,2048]{0,1:T(8,128)S(1)}, f32[128,2048]{0,1:T(8,128)S(1)}, u32[]{:S(2)}, u32[]{:S(2)}) %collective-permute-start.1) | collective-permute-done | bytes 1048608 | tf_op jit(solution)/shard_map/ppermute | solution.py:10
  82.5 1.2 slice_add_fusion
  83.7 1.6 copy.39
  85.3 2.5 %fusion.8 = (bf16[1,128,2048]{2,1,0:T(8,128)(2,1)}, bf16[1,128,2048]{2,1,0:T(8,128)(2,1)}, bf16[1,128,2048]{2,1,0:T(8,128)(2,1)S(1)}) fusion(f32[1,128,2048]{2,1,0:T(8,128)S(1)} %copy.39, bf16[1,128,2048]{2,1,0:T(8,128)(2,1)} %param.7, bf16[1,128,2048]{2,1,0:T(8,128)(2,1)} %param.8), kind=kLoop, calls=%fused_computation.13 | loop fusion | flops 2097152 | bytes 3670016 | tf_op jit(solution)/shard_map/convert_element_type | solution.py:119
  87.8 2.1 collective-permute-start
  89.9 0.3 copy.37
  90.2 5.6 %collective-permute-done = bf16[128,2048]{1,0:T(8,128)(2,1)S(1)} collective-permute-done((bf16[128,2048]{1,0:T(8,128)(2,1)S(1)}, bf16[128,2048]{1,0:T(8,128)(2,1)S(1)}, u32[]{:S(2)}, u32[]{:S(2)}) %collective-permute-start) | collective-permute-done | bytes 524320 | tf_op jit(solution)/shard_map/ppermute | solution.py:10
  95.9 0.3 copy.36
  96.1 2.4 %fusion.13 = f32[128,128,256]{2,1,0:T(8,128)S(1)} fusion(bf16[128,128,16]{0,2,1:T(8,128)(2,1)S(1)} %bitcast.43, bf16[1,128,128,16]{1,3,2,0:T(8,128)(2,1)S(1)} %bitcast.38, bf16[1,128,128,16]{1,3,2,0:T(8,128)(2,1)S(1)} %bitcast.40), kind=kOutput, calls=%fused_computation.21 | convolution fusion | flops 136314880 | bytes 18350080 | tf_op jit(solution)/shard_map/btfc,bjfc->ftj/dot_general | solution.py:120
  98.5 8.9 %pad.8 = f32[128,128,383]{2,1,0:T(8,128)} pad(f32[128,128,256]{2,1,0:T(8,128)S(1)} %fusion.13, f32[]{:T(128)} %constant.3.clone.1), padding=0_0x0_0x0_127 | pad | bytes 41877508 | tf_op jit(solution)/shard_map/jit(_pad)/pad | solution.py:70
  107.4 26.8 %reshape.125 = f32[128,49024]{1,0:T(8,128)} reshape(f32[128,128,383]{2,1,0:T(8,128)} %pad.8) | data formatting | bytes 50200576 | tf_op jit(solution)/shard_map/reshape | solution.py:71
  134.2 11.7 %pad.9 = f32[128,49152]{1,0:T(8,128)S(1)} pad(f32[128,49024]{1,0:T(8,128)} %reshape.125, f32[]{:T(128)} %constant.3.clone.1), padding=0_0x127_1 | pad | bytes 50266116 | tf_op jit(solution)/shard_map/jit(_pad)/pad | solution.py:72
  145.9 10.4 %copy.46 = f32[16,8,128,384]{3,2,1,0:T(8,128)} copy(f32[16,8,128,384]{3,1,2,0:T(8,128)S(1)} %bitcast.35) | data formatting | bytes 50331648
  156.3 9.5 %bitcast_reduce_fusion = f32[128,384]{1,0:T(8,128)S(1)} fusion(f32[16,8,128,384]{3,2,1,0:T(8,128)} %copy.46), kind=kLoop, calls=%fused_computation | loop fusion | flops 6242304 | bytes 25362432 | tf_op jit(solution)/shard_map/reduce_sum | solution.py:73
  165.8 0.1 rev.7
  165.9 25.3 %all_to_all.15 = f32[64,2,128]{2,1,0:T(2,128)S(1)} all-to-all(f32[64,2,128]{2,1,0:T(2,128)S(1)} %bitcast.49), channel_id=1, replica_groups=mesh['dp'=4,'ctx'=64] {'ctx'}, dimensions={0} | all-to-all | bytes 131072 | tf_op jit(solution)/shard_map/all_to_all | solution.py:20
  191.2 0.1 reduce_sum.28
  191.3 0.7 broadcast_in_dim.27
  191.9 4.4 %all-to-all-start.1 = ((f32[64,2,128]{2,1,0:T(2,128)}), f32[64,2,128]{2,1,0:T(2,128)S(1)}, u32[]{:S(2)}, u32[]{:S(2)}) async-start(f32[64,2,128]{2,1,0:T(2,128)} %broadcast_in_dim.27), calls=%async_computation.1 | async-start | bytes 131072 | tf_op jit(solution)/shard_map/all_to_all | solution.py:37
  196.4 5.7 %fusion.2 = f32[128,16,128]{2,1,0:T(8,128)S(1)} fusion(bf16[128,128,383]{2,1,0:T(8,128)(2,1)} %reshape.122, bf16[1,128,128,16]{1,3,2,0:T(8,128)(2,1)S(1)} %bitcast.39, bf16[1,128,128,16]{1,3,2,0:T(8,128)(2,1)S(1)} %bitcast.41), kind=kOutput, calls=%fused_computation.3 | convolution fusion | flops 136314880 | bytes 10485760 | tf_op jit(solution)/shard_map/ftj,bjfc->btfc/dot_general | solution.py:105
  202.0 4.4 %all-to-all-done.1 = f32[64,2,128]{2,1,0:T(2,128)S(1)} async-done(((f32[64,2,128]{2,1,0:T(2,128)}), f32[64,2,128]{2,1,0:T(2,128)S(1)}, u32[]{:S(2)}, u32[]{:S(2)}) %all-to-all-start.1) | async-done | bytes 65568 | tf_op jit(solution)/shard_map/all_to_all | solution.py:37
  206.5 0.7 broadcast_in_dim.28
  207.2 4.2 %all-to-all-start.2 = ((f32[4,128,128]{2,1,0:T(8,128)}), f32[4,128,128]{2,1,0:T(8,128)S(1)}, u32[]{:S(2)}, u32[]{:S(2)}) async-start(f32[4,128,128]{2,1,0:T(8,128)} %broadcast_in_dim.28), calls=%async_computation.2 | async-start | bytes 524288 | tf_op jit(solution)/shard_map/all_to_all | solution.py:37
  211.4 0.2 fusion.11
  211.6 1.0 copy.43
  212.6 1.0 copy.42
  213.6 3.6 %all-to-all-done.2 = f32[4,128,128]{2,1,0:T(8,128)S(1)} async-done(((f32[4,128,128]{2,1,0:T(8,128)}), f32[4,128,128]{2,1,0:T(8,128)S(1)}, u32[]{:S(2)}, u32[]{:S(2)}) %all-to-all-start.2) | async-done | bytes 262176 | tf_op jit(solution)/shard_map/all_to_all | solution.py:37
  217.2 0.6 reduce_sum.29
  (6 shorter events, 0.1 us)
Async XLA Ops:
  65.6 17.0 %collective-permute-start.1 = (f32[128,2048]{0,1:T(8,128)S(1)}, f32[128,2048]{0,1:T(8,128)S(1)}, u32[]{:S(2)}, u32[]{:S(2)}) collective-permute-start(f32[128,2048]{0,1:T(8,128)S(1)} %bitcast.47), channel_id=1, source_target_pairs={{1,0},{2,1},{3,2},{4,3},{5,4},{6,5},{7,6},{8,7},{9,8},{10,9},{11,1... | collective-permute-start | bytes 3145736 | tf_op jit(solution)/shard_map/ppermute | solution.py:10
  87.8 8.0 %collective-permute-start = (bf16[128,2048]{1,0:T(8,128)(2,1)S(1)}, bf16[128,2048]{1,0:T(8,128)(2,1)S(1)}, u32[]{:S(2)}, u32[]{:S(2)}) collective-permute-start(bf16[128,2048]{1,0:T(8,128)(2,1)S(1)} %bitcast.45), channel_id=1, source_target_pairs={{0,1},{1,2},{2,3},{3,4},{4,5},{5,6},{6,7},{7,8},{8,9},{9,10},{10,1... | collective-permute-start | bytes 1572872 | tf_op jit(solution)/shard_map/ppermute | solution.py:10
  191.9 14.6 %all-to-all-start.1 = ((f32[64,2,128]{2,1,0:T(2,128)}), f32[64,2,128]{2,1,0:T(2,128)S(1)}, u32[]{:S(2)}, u32[]{:S(2)}) async-start(f32[64,2,128]{2,1,0:T(2,128)} %broadcast_in_dim.27), calls=%async_computation.1 | async-start | bytes 131072 | tf_op jit(solution)/shard_map/all_to_all | solution.py:37
  207.2 10.0 %all-to-all-start.2 = ((f32[4,128,128]{2,1,0:T(8,128)}), f32[4,128,128]{2,1,0:T(8,128)S(1)}, u32[]{:S(2)}, u32[]{:S(2)}) async-start(f32[4,128,128]{2,1,0:T(8,128)} %broadcast_in_dim.28), calls=%async_computation.2 | async-start | bytes 524288 | tf_op jit(solution)/shard_map/all_to_all | solution.py:37
where the time goes:
time: 219 us; the launch traced here: 218 us
  local copies, waits for them, and re-layouts  122 us (56%)
  waiting for transfers between devices  25.5 us (12%)
  blocking collectives  25.3 us (12%)
  starting transfers between devices  15.8 us (7%)
  other arithmetic  15.3 us (7%)
  matrix products  12.6 us (6%)
    reshape x1, local copies, waits for them, and re-layouts, build_tiles(): flattened.reshape(group_count, tap_count, stride)[:, :, :2 * tap_count]  30.8 us
    unnamed x6, local copies, waits for them, and re-layouts  27.5 us
    reshape x1, local copies, waits for them, and re-layouts, diagonal_sums(): flattened = padded.reshape(group_count, tap_count * stride)  26.8 us
    all_to_all x1, blocking collectives, summed_on_arrival(): lax.all_to_all(tiles, axis, split_axis=0, concat_axis=0, tiled=True)  25.3 us
    ppermute x2, waiting for transfers between devices, shifted(): return lax.ppermute(array, axis, pairs)  17.5 us
    pad x1, local copies, waits for them, and re-layouts, diagonal_sums(): flattened = jnp.pad(flattened, ((0, 0), (tap_count - 1, 1)))  11.7 us
    reduce_sum x1, other arithmetic, diagonal_sums(): jnp.sum(flattened.reshape(group_count, tap_count, 3 * tap_count), axis=1)  9.48 us
    pad x1, local copies, waits for them, and re-layouts, diagonal_sums(): padded = jnp.pad(tile_grads, ((0, 0), (0, 0), (0, stride - 2 * tap_count)))  8.9 us
  transfers between devices with their start and end apart: 4, of which 4 were waited for; matrix products, arithmetic and copies ran while one was open for 4% of the time, Pallas kernels for 0%

commit v1 on v0

v1 whole, which is shorter than its diff:
```python
import functools

import jax
import jax.numpy as jnp
from jax import lax
from jax.experimental import pallas as pl
from jax.experimental.pallas import tpu as pltpu
from jax.sharding import PartitionSpec as P

F32, BF16 = jnp.float32, jnp.bfloat16
MESH = pl.DeviceIdType.MESH
NT = (((1,), (1,)), ((), ()))


def build_bases(h_ref, hs_ref, b1_ref, b2_ref):
    lane = lax.broadcasted_iota(jnp.int32, (128, 128), 1)
    sub = lax.broadcasted_iota(jnp.int32, (128, 128), 0)
    flip = (lane + sub == 127).astype(BF16)
    h = h_ref[...]
    hs_ref[0] = h.astype(F32)
    hs_ref[1] = jnp.dot(h, flip, preferred_element_type=F32)
    r = lax.broadcasted_iota(jnp.int32, (16, 128), 0)
    m = lax.broadcasted_iota(jnp.int32, (16, 128), 1)

    def step(i, _):
        for j in range(8):
            f = i * 8 + j
            rows = pl.ds(pl.multiple_of(f * 16, 16), 16)
            fwd = jnp.broadcast_to(hs_ref[0, pl.ds(f, 1), :], (16, 128))
            rev = jnp.broadcast_to(hs_ref[1, pl.ds(f, 1), :], (16, 128))
            fwd = pltpu.roll(fwd, 0, 1, stride=1, stride_axis=0)
            rev = pltpu.roll(rev, 1, 1, stride=1, stride_axis=0)
            b2_ref[rows, 0:128] = jnp.where(m >= r, fwd, 0.0).astype(BF16)
            b2_ref[rows, 128:256] = jnp.where(m < r, fwd, 0.0).astype(BF16)
            b1_ref[rows, 0:128] = jnp.where(m >= r + 1, rev, 0.0).astype(BF16)
            b1_ref[rows, 128:256] = jnp.where(m < r + 1, rev, 0.0).astype(BF16)
        return 0

    lax.fori_loop(0, 16, step, 0)


def pick(full, half, group):
    lanes = slice(128 * half, 128 * half + 128)
    out = full[112:128, lanes]
    for g in range(6, -1, -1):
        out = jnp.where(group == g, full[16 * g : 16 * g + 16, lanes], out)
    return out


def slab(ref, a, blk):
    return jnp.concatenate(
        [ref[16 * a : 16 * a + 144, blk], ref[16 * a + 16 : 16 * a + 160, blk]], axis=1
    )


def block_of(i):
    return pl.ds(pl.multiple_of(i * 128, 128), 128)


def lane_group():
    return lax.broadcasted_iota(jnp.int32, (16, 128), 1) // 16


def conv_block(i, q_ref, k_ref, v_ref, c_ref, u_ref, d_ref, b1_ref, b2_ref, outs):
    z_ref, gq_ref, gk_ref, gv_ref = outs
    blk = block_of(i)
    group = lane_group()
    lhs1 = b1_ref[blk, 0:144]
    lhs2 = b2_ref[blk, 0:144]
    for a in range(0, 8, 2):
        y = jnp.dot(lhs1, slab(u_ref, a, blk), preferred_element_type=F32)
        du = jnp.dot(lhs2, slab(d_ref, a, blk), preferred_element_type=F32)
        for half in range(2):
            rows = slice(16 * (a + half), 16 * (a + half) + 16)
            yv = pick(y, half, group)
            z_ref[rows, blk] = (q_ref[rows, blk].astype(F32) * yv).astype(BF16)
            gq_ref[rows, blk] = (c_ref[rows, blk].astype(F32) * yv).astype(BF16)
            dv = pick(du, half, group)
            gk_ref[rows, blk] = (v_ref[rows, blk].astype(F32) * dv).astype(BF16)
            gv_ref[rows, blk] = (k_ref[rows, blk].astype(F32) * dv).astype(BF16)


def pair_sums(i, u_ref, d_ref, g_ref):
    blk = block_of(i)
    group = lane_group()
    total = jnp.zeros((128, 144), F32)
    for a in range(0, 8, 2):
        pair = []
        for half in range(2):
            start = 128 + 16 * (a + half)
            rows = u_ref[start : start + 16, blk]
            spread = [jnp.where(group == g, rows, jnp.zeros_like(rows)) for g in range(8)]
            pair.append(jnp.concatenate(spread, axis=0))
        total = total + lax.dot_general(
            jnp.concatenate(pair, axis=1), slab(d_ref, a, blk), NT, preferred_element_type=F32
        )
    g_ref[blk, 0:144] = total


def diagonals(i, g_ref):
    rows = block_of(i)
    lane = lax.broadcasted_iota(jnp.int32, (128, 128), 1)
    r = lax.broadcasted_iota(jnp.int32, (128, 128), 0) % 16
    both = jnp.where(lane < r, g_ref[rows, 128:256], g_ref[rows, 0:128])
    parts = [
        both[16 * f : 16 * f + 8] + pltpu.roll(both[16 * f + 8 : 16 * f + 16], 120, 1)
        for f in range(8)
    ]
    sub = lax.broadcasted_iota(jnp.int32, (8, 128), 0)
    for step in (4, 2, 1):
        low = sub % (2 * step) < step
        merged = []
        for f in range(step):
            one, two = parts[f], parts[f + step]
            first = jnp.where(low, one, pltpu.roll(two, step, 0))
            second = jnp.where(low, pltpu.roll(one, 8 - step, 0), two)
            merged.append(first + pltpu.roll(second, 128 - step, 1))
        parts = merged
    return parts[0]


def tile_kernel(h_ref, q_ref, k_ref, v_ref, c_ref, up_ref, dn_ref,
                z_ref, gq_ref, gk_ref, gv_ref, fg_ref,
                u_ref, d_ref, b1_ref, b2_ref, hs_ref, g_ref):
    build_bases(h_ref, hs_ref, b1_ref, b2_ref)
    u_ref[0:128] = up_ref[...]
    d_ref[128:256] = dn_ref[...]
    u_ref[128:256] = (k_ref[...].astype(F32) * v_ref[...].astype(F32)).astype(BF16)
    d_ref[0:128] = (c_ref[...].astype(F32) * q_ref[...].astype(F32)).astype(BF16)
    outs = (z_ref, gq_ref, gk_ref, gv_ref)

    def step(i, _):
        pair_sums(i, u_ref, d_ref, g_ref)
        conv_block(i, q_ref, k_ref, v_ref, c_ref, u_ref, d_ref, b1_ref, b2_ref, outs)
        return 0

    lax.fori_loop(0, 16, step, 0)

    def last(i, _):
        for j in range(4):
            rows = diagonals(4 * i + j, g_ref)
            fg_ref[8 * i + 2 * j] = rows[0:4]
            fg_ref[8 * i + 2 * j + 1] = rows[4:8]
        return 0

    lax.fori_loop(0, 4, last, 0)


def tile_ops(h, q, k, v, c, up, dn):
    sd = jax.ShapeDtypeStruct
    vmem = pl.BlockSpec(memory_space=pltpu.VMEM)
    return pl.pallas_call(
        tile_kernel,
        out_shape=[sd((128, 2048), BF16)] * 4 + [sd((32, 4, 128), F32)],
        in_specs=[vmem] * 7,
        out_specs=[vmem] * 5,
        scratch_shapes=[pltpu.VMEM((256, 2048), BF16)] * 2
        + [pltpu.VMEM((2048, 256), BF16)] * 2
        + [pltpu.VMEM((2, 128, 128), F32), pltpu.VMEM((2048, 256), F32)],
        name="tile_ops",
    )(h, q, k, v, c, up, dn)


def reduce_everywhere(fg_ref, put_ref, rs_buf, z_buf, part, sems):
    rs_send, rs_recv, z_send, z_recv, ag_send, ag_recv = sems
    ctx = lax.axis_index("ctx")
    own = lax.axis_index("dp") * 8 + lax.rem(ctx, 8)
    z = ctx // 8

    def plane(k):
        p = lax.rem(own + k, 32)
        return p, {"dp": p // 8, "ctx": z * 8 + lax.rem(p, 8)}

    def along(k):
        p = lax.rem(z + k, 8)
        return p, {"ctx": p * 8 + lax.rem(ctx, 8)}

    def rs(k):
        p, where = plane(k)
        return p, pltpu.make_async_remote_copy(
            fg_ref.at[p], rs_buf.at[own], rs_send.at[k], rs_recv.at[own], where, MESH)

    def rs_in(k):
        p, where = plane(k)
        return pltpu.make_async_remote_copy(
            fg_ref.at[p], rs_buf.at[p], rs_send.at[k], rs_recv.at[p], where, MESH)

    def ar(k):
        p, where = along(k)
        return pltpu.make_async_remote_copy(
            part.at[0], z_buf.at[z], z_send.at[k], z_recv.at[z], where, MESH)

    def ar_in(k):
        p, where = along(k)
        return pltpu.make_async_remote_copy(
            part.at[0], z_buf.at[p], z_send.at[k], z_recv.at[p], where, MESH)

    def ag(k):
        p, where = plane(k)
        return pltpu.make_async_remote_copy(
            part.at[1], put_ref.at[own], ag_send.at[k], ag_recv.at[own], where, MESH)

    def ag_in(k):
        p, where = plane(k)
        return pltpu.make_async_remote_copy(
            part.at[1], put_ref.at[p], ag_send.at[k], ag_recv.at[p], where, MESH)

    def each(lo, hi, what):
        def body(k, _):
            what(k)
            return 0
        lax.fori_loop(lo, hi, body, 0)

    each(1, 32, lambda k: rs(k)[1].start())
    rs_buf[own] = fg_ref[own]
    each(1, 32, lambda k: rs_in(k).wait_recv())
    total = rs_buf[0]
    for p in range(1, 32):
        total = total + rs_buf[p]
    part[0] = total
    each(1, 8, lambda k: ar(k).start())
    z_buf[z] = total
    each(1, 8, lambda k: ar_in(k).wait_recv())
    total = z_buf[0]
    for p in range(1, 8):
        total = total + z_buf[p]
    part[1] = total
    each(1, 32, lambda k: ag(k).start())
    put_ref[own] = total
    each(1, 32, lambda k: ag_in(k).wait_recv())
    each(1, 32, lambda k: rs(k)[1].wait_send())
    each(1, 8, lambda k: ar(k).wait_send())
    each(1, 32, lambda k: ag(k).wait_send())


def greet_reducers():
    barrier = pltpu.get_barrier_semaphore()
    ctx = lax.axis_index("ctx")
    own = lax.axis_index("dp") * 8 + lax.rem(ctx, 8)
    z = ctx // 8

    def plane(k, _):
        p = lax.rem(own + k, 32)
        pl.semaphore_signal(barrier, 1, device_id={"dp": p // 8, "ctx": z * 8 + lax.rem(p, 8)}, device_id_type=MESH)
        return 0

    def along(k, _):
        p = lax.rem(z + k, 8)
        pl.semaphore_signal(barrier, 1, device_id={"ctx": p * 8 + lax.rem(ctx, 8)}, device_id_type=MESH)
        return 0

    lax.fori_loop(1, 32, plane, 0)
    lax.fori_loop(1, 8, along, 0)
    return barrier


AR_SCRATCH = [
    pltpu.VMEM((32, 4, 128), F32),
    pltpu.VMEM((8, 4, 128), F32),
    pltpu.VMEM((2, 4, 128), F32),
] + [pltpu.SemaphoreType.DMA((n,)) for n in (32, 32, 8, 8, 32, 32)]


def sum_kernel(fg_ref, put_ref, rs_buf, z_buf, part, *sems):
    barrier = greet_reducers()
    pl.semaphore_wait(barrier, 38)
    reduce_everywhere(fg_ref, put_ref, rs_buf, z_buf, part, sems)


def sum_everywhere(fg):
    vmem = pl.BlockSpec(memory_space=pltpu.VMEM)
    return pl.pallas_call(
        sum_kernel,
        out_shape=jax.ShapeDtypeStruct((32, 4, 128), F32),
        in_specs=[vmem],
        out_specs=vmem,
        scratch_shapes=AR_SCRATCH,
        compiler_params=pltpu.CompilerParams(collective_id=0, has_side_effects=True),
        name="sum_everywhere",
    )(fg)


def keeps(starts, ctx):
    own = jnp.any(starts == ctx * 128)
    after = jnp.any(starts == (ctx + 1) * 128) | (ctx == 63)
    return jnp.where(own, 0.0, 1.0).astype(BF16), jnp.where(after, 0.0, 1.0).astype(BF16)


def per_device(gate_in, key_in, value_in, cotangent, doc_starts, filters):
    q, k, v, c = gate_in[0], key_in[0], value_in[0], cotangent[0]
    keep_own, keep_after = keeps(doc_starts[0], lax.axis_index("ctx"))
    u = (k.astype(F32) * v.astype(F32)).astype(BF16) * keep_after
    dy = (c.astype(F32) * q.astype(F32)).astype(BF16) * keep_own
    up = lax.ppermute(u, "ctx", [(i, (i + 1) % 64) for i in range(64)])
    dn = lax.ppermute(dy, "ctx", [(i, (i - 1) % 64) for i in range(64)])
    z, gq, gk, gv, fg = tile_ops(filters, q, k, v, c, up, dn)
    total = sum_everywhere(fg).reshape(128, 128)
    return z[None], gq[None], gk[None], gv[None], total


def solution(mesh):
    rows = P("dp", "ctx", None)
    return jax.shard_map(
        per_device,
        mesh=mesh,
        in_specs=(rows, rows, rows, rows, P("dp", None), P()),
        out_specs=(rows, rows, rows, rows, P()),
        check_vma=False,
    )
```

time: 219 us -> 60.1 us (0.27)
  local copies, waits for them, and re-layouts: 122 us -> 2.92 us
  Pallas kernels: 0 us -> 41 us
  blocking collectives: 25.3 us -> 0 us
  waiting for transfers between devices: 25.5 us -> 8.28 us
  other arithmetic: 15.3 us -> 2.24 us
  matrix products: 12.6 us -> 0 us
  starting transfers between devices: 15.8 us -> 3.36 us
    reshape x3 -> x0, local copies, waits for them, and re-layouts: 59.1 us -> none  [the longest x1 30.8 us: build_tiles(): flattened.reshape(group_count, tap_count, stride)[:, :, :2 * tap_count]]
    pallas_call x0 -> x2, Pallas kernels: none -> 41 us  [the longest x1 28.8 us: sum_everywhere(): pl.pallas_call(sum_kernel, out_shape=jax.ShapeDtypeStruct((32, 4, 128), F...]
    all_to_all x1 -> x0, blocking collectives: 25.3 us -> none  [summed_on_arrival(): lax.all_to_all(tiles, axis, split_axis=0, concat_axis=0, tiled=True)]
    unnamed x6 -> x11, local copies, waits for them, and re-layouts: 27.5 us -> 2.92 us
    pad x2 -> x0, local copies, waits for them, and re-layouts: 20.6 us -> none  [the longest x1 11.7 us: diagonal_sums(): flattened = jnp.pad(flattened, ((0, 0), (tap_count - 1, 1)))]
    dot_general x3 -> x0, matrix products: 12.6 us -> none  [the longest x1 5.66 us: per_device(): jnp.einsum('ftj,bjfc->btfc', toeplitz, window, preferred_element_type=jnp...]
    reduce_sum x3 -> x0, other arithmetic: 10.2 us -> none  [the longest x1 9.48 us: diagonal_sums(): jnp.sum(flattened.reshape(group_count, tap_count, 3 * tap_count), axis=1)]
    ppermute x2, waiting for transfers between devices: 17.5 us -> 8.28 us  [the longest x1 4.58 us: per_device(): up = lax.ppermute(u, 'ctx', [(i, (i + 1) % 64) for i in range(64)])]
  transfers between devices with their start and end apart: 4 -> 2, of which waited for: 4 -> 2; matrix products, arithmetic and copies ran while one was open for 4% -> 0% of each run, Pallas kernels for 0% -> 0%
where the time goes in v1:
time: 60.1 us; the launch traced here: 59.8 us
  Pallas kernels  41 us (68%)
  waiting for transfers between devices  8.28 us (14%)
  starting transfers between devices  3.36 us (6%)
  local copies, waits for them, and re-layouts  2.92 us (5%)
  other arithmetic  2.24 us (4%)
  between operations  2.02 us (3%)
    pallas_call x1, Pallas kernels, sum_everywhere(): pl.pallas_call(sum_kernel, out_shape=jax.ShapeDtypeStruct((32, 4, 128), F...  28.8 us
    pallas_call x1, Pallas kernels, tile_ops(): pl.pallas_call(tile_kernel, out_shape=[sd((128, 2048), BF16)] * 4 + [sd((...  12.2 us
    ppermute x1, waiting for transfers between devices, per_device(): up = lax.ppermute(u, 'ctx', [(i, (i + 1) % 64) for i in range(64)])  4.58 us
    ppermute x1, waiting for transfers between devices, per_device(): dn = lax.ppermute(dy, 'ctx', [(i, (i - 1) % 64) for i in range(64)])  3.7 us
    unnamed x11, local copies, waits for them, and re-layouts  2.92 us
    ppermute x1, starting transfers between devices, per_device(): up = lax.ppermute(u, 'ctx', [(i, (i + 1) % 64) for i in range(64)])  2.67 us
    mul x1, other arithmetic, per_device(): u = (k.astype(F32) * v.astype(F32)).astype(BF16) * keep_after  1.45 us
  transfers between devices with their start and end apart: 2, of which 2 were waited for; matrix products, arithmetic and copies ran while one was open for 0% of the time, Pallas kernels for 0%

profile of v1, /device:TPU:1, one launch (start us, length us, event | category | flops | bytes accessed | tf_op | source)
XLA Modules:
  0.0 59.8 jit_solution(5781296348910934064)
XLA Ops:
  0.6 0.0 copy-start.4
  0.6 0.6 %copy-done.4 = s32[1,17]{1,0:T(1,128)S(1)} copy-done((s32[1,17]{1,0:T(1,128)S(1)}, s32[1,17]{1,0:T(1,128)}, u32[]{:S(2)}) %copy-start.4) | copy-done | bytes 92
  1.3 0.6 %compare_reduce_fusion = (pred[]{:T(512)}, pred[]{:T(512)}) fusion(s32[1,17]{1,0:T(1,128)S(1)} %copy-done.4, s32[]{:T(128)S(6)} %mul.29, s32[]{:T(128)S(6)} %mul.25), kind=kLoop, calls=%fused_computation.4 | loop fusion | flops 66 | bytes 78 | tf_op jit(solution)/shard_map/reduce_or | solution.py:284
  2.6 0.0 copy-start
  2.6 0.0 copy-start.1
  2.6 1.4 %fusion = bf16[128,2048]{1,0:T(8,128)(2,1)S(1)} fusion(bf16[]{:T(256)S(6)} %select_n.7, bf16[1,128,2048]{2,1,0:T(8,128)(2,1)} %param.8, bf16[1,128,2048]{2,1,0:T(8,128)(2,1)} %param.7), kind=kLoop, calls=%fused_computation.2 | loop fusion | flops 1310720 | bytes 1572866 | tf_op jit(solution)/shard_map/mul | solution.py:292
  4.1 2.7 %collective-permute-start = (bf16[128,2048]{1,0:T(8,128)(2,1)S(1)}, bf16[128,2048]{1,0:T(8,128)(2,1)S(1)}, u32[]{:S(2)}, u32[]{:S(2)}) collective-permute-start(bf16[128,2048]{1,0:T(8,128)(2,1)S(1)} %fusion), channel_id=1, source_target_pairs={{0,1},{1,2},{2,3},{3,4},{4,5},{5,6},{6,7},{7,8},{8,9},{9,10},{10,1... | collective-permute-start | bytes 1572872 | tf_op jit(solution)/shard_map/ppermute | solution.py:294
  7.4 0.0 copy-done
  7.4 0.0 copy-done.1
  7.4 0.2 fusion.1
  7.6 0.7 %collective-permute-start.1 = (bf16[128,2048]{1,0:T(8,128)(2,1)S(1)}, bf16[128,2048]{1,0:T(8,128)(2,1)S(1)}, u32[]{:S(2)}, u32[]{:S(2)}) collective-permute-start(bf16[128,2048]{1,0:T(8,128)(2,1)S(1)} %fusion.1), channel_id=1, source_target_pairs={{0,63},{1,0},{2,1},{3,2},{4,3},{5,4},{6,5},{7,6},{8,7},{9,8},{10,9... | collective-permute-start | bytes 1572872 | tf_op jit(solution)/shard_map/ppermute | solution.py:295
  8.3 4.6 %collective-permute-done.up_ref = bf16[128,2048]{1,0:T(8,128)(2,1)S(1)} collective-permute-done((bf16[128,2048]{1,0:T(8,128)(2,1)S(1)}, bf16[128,2048]{1,0:T(8,128)(2,1)S(1)}, u32[]{:S(2)}, u32[]{:S(2)}) %collective-permute-start) | collective-permute-done | bytes 524320 | tf_op jit(solution)/shard_map/ppermute | solution.py:294
  12.9 0.0 copy-start.2
  12.9 3.7 %collective-permute-done.1.dn_ref = bf16[128,2048]{1,0:T(8,128)(2,1)S(1)} collective-permute-done((bf16[128,2048]{1,0:T(8,128)(2,1)S(1)}, bf16[128,2048]{1,0:T(8,128)(2,1)S(1)}, u32[]{:S(2)}, u32[]{:S(2)}) %collective-permute-start.1) | collective-permute-done | bytes 524320 | tf_op jit(solution)/shard_map/ppermute | solution.py:295
  16.6 0.0 copy-start.3
  16.6 0.0 copy-done.2
  16.6 0.8 %copy-done.3 = bf16[128,2048]{1,0:T(8,128)(2,1)} copy-done((bf16[128,2048]{1,0:T(8,128)(2,1)}, bf16[128,2048]{1,0:T(8,128)(2,1)S(1)}, u32[]{:S(2)}) %copy-start.3) | copy-done | bytes 524312
  17.3 12.2 %tile_ops.1 = (bf16[128,2048]{1,0:T(8,128)(2,1)}, bf16[128,2048]{1,0:T(8,128)(2,1)}, bf16[128,2048]{1,0:T(8,128)(2,1)}, bf16[128,2048]{1,0:T(8,128)(2,1)}, f32[32,4,128]{2,1,0:T(4,128)}) custom-call(bf16[128,128]{1,0:T(8,128)(2,1)} %h_ref.1, bf16[128,2048]{1,0:T(8,128)(2,1)} %bitcast.13, bf16[128,2048]{1,0:T(8,128)(2,1)} %bitcast.14, ...), custom_call_target="tpu_custom_call" | custom-call | tf_op jit(solution)/shard_map/tile_ops/pallas_call | solution.py:152
  29.5 28.8 %sum_everywhere.1 = f32[32,4,128]{2,1,0:T(4,128)} custom-call(f32[32,4,128]{2,1,0:T(4,128)} %get-tuple-element.14.fg_ref), custom_call_target="tpu_custom_call" | custom-call | tf_op jit(solution)/shard_map/sum_everywhere/pallas_call | solution.py:272
  58.4 1.5 %copy.12 = f32[128,128]{1,0:T(8,128)} copy(f32[128,128]{1,0:T(8,128)} %bitcast.17) | data formatting | bytes 131072
Async XLA Ops:
  0.6 0.7 %copy-start.4 = (s32[1,17]{1,0:T(1,128)S(1)}, s32[1,17]{1,0:T(1,128)}, u32[]{:S(2)}) copy-start(s32[1,17]{1,0:T(1,128)} %param.10) | copy-start | bytes 208
  2.6 4.8 %copy-start = (bf16[1,128,2048]{2,1,0:T(8,128)(2,1)S(1)}, bf16[1,128,2048]{2,1,0:T(8,128)(2,1)}, u32[]{:S(2)}) copy-start(bf16[1,128,2048]{2,1,0:T(8,128)(2,1)} %param.6) | copy-start | bytes 1572868
  2.6 4.8 %copy-start.1 = (bf16[1,128,2048]{2,1,0:T(8,128)(2,1)S(1)}, bf16[1,128,2048]{2,1,0:T(8,128)(2,1)}, u32[]{:S(2)}) copy-start(bf16[1,128,2048]{2,1,0:T(8,128)(2,1)} %param.9) | copy-start | bytes 1572868
  4.1 8.8 %collective-permute-start = (bf16[128,2048]{1,0:T(8,128)(2,1)S(1)}, bf16[128,2048]{1,0:T(8,128)(2,1)S(1)}, u32[]{:S(2)}, u32[]{:S(2)}) collective-permute-start(bf16[128,2048]{1,0:T(8,128)(2,1)S(1)} %fusion), channel_id=1, source_target_pairs={{0,1},{1,2},{2,3},{3,4},{4,5},{5,6},{6,7},{7,8},{8,9},{9,10},{10,1... | collective-permute-start | bytes 1572872 | tf_op jit(solution)/shard_map/ppermute | solution.py:294
  7.6 9.0 %collective-permute-start.1 = (bf16[128,2048]{1,0:T(8,128)(2,1)S(1)}, bf16[128,2048]{1,0:T(8,128)(2,1)S(1)}, u32[]{:S(2)}, u32[]{:S(2)}) collective-permute-start(bf16[128,2048]{1,0:T(8,128)(2,1)S(1)} %fusion.1), channel_id=1, source_target_pairs={{0,63},{1,0},{2,1},{3,2},{4,3},{5,4},{6,5},{7,6},{8,7},{9,8},{10,9... | collective-permute-start | bytes 1572872 | tf_op jit(solution)/shard_map/ppermute | solution.py:295
  12.9 3.7 %copy-start.2 = (bf16[128,2048]{1,0:T(8,128)(2,1)}, bf16[128,2048]{1,0:T(8,128)(2,1)S(1)}, u32[]{:S(2)}) copy-start(bf16[128,2048]{1,0:T(8,128)(2,1)S(1)} %collective-permute-done.up_ref) | copy-start | bytes 1572868
  16.6 0.8 %copy-start.3 = (bf16[128,2048]{1,0:T(8,128)(2,1)}, bf16[128,2048]{1,0:T(8,128)(2,1)S(1)}, u32[]{:S(2)}) copy-start(bf16[128,2048]{1,0:T(8,128)(2,1)S(1)} %collective-permute-done.1.dn_ref) | copy-start | bytes 1572868

commit v2 on v1

v2 whole, which is shorter than its diff:
```python
import itertools

import jax
import jax.numpy as jnp
from jax import lax
from jax.experimental import pallas as pl
from jax.experimental.pallas import tpu as pltpu
from jax.sharding import PartitionSpec as P

F32, BF16 = jnp.float32, jnp.bfloat16
MESH = pl.DeviceIdType.MESH
NT = (((1,), (1,)), ((), ()))


def build_bases(h_ref, hs_ref, b1_ref, b2_ref):
    lane = lax.broadcasted_iota(jnp.int32, (128, 128), 1)
    sub = lax.broadcasted_iota(jnp.int32, (128, 128), 0)
    flip = (lane + sub == 127).astype(BF16)
    h = h_ref[...]
    hs_ref[0] = h.astype(F32)
    hs_ref[1] = jnp.dot(h, flip, preferred_element_type=F32)
    r = lax.broadcasted_iota(jnp.int32, (16, 128), 0)
    m = lax.broadcasted_iota(jnp.int32, (16, 128), 1)

    def step(i, _):
        for j in range(8):
            f = i * 8 + j
            rows = pl.ds(pl.multiple_of(f * 16, 16), 16)
            fwd = jnp.broadcast_to(hs_ref[0, pl.ds(f, 1), :], (16, 128))
            rev = jnp.broadcast_to(hs_ref[1, pl.ds(f, 1), :], (16, 128))
            fwd = pltpu.roll(fwd, 0, 1, stride=1, stride_axis=0)
            rev = pltpu.roll(rev, 1, 1, stride=1, stride_axis=0)
            b2_ref[rows, 0:128] = jnp.where(m >= r, fwd, 0.0).astype(BF16)
            b2_ref[rows, 128:256] = jnp.where(m < r, fwd, 0.0).astype(BF16)
            b1_ref[rows, 0:128] = jnp.where(m >= r + 1, rev, 0.0).astype(BF16)
            b1_ref[rows, 128:256] = jnp.where(m < r + 1, rev, 0.0).astype(BF16)
        return 0

    lax.fori_loop(0, 16, step, 0)


def pick(full, half, group):
    lanes = slice(128 * half, 128 * half + 128)
    out = full[112:128, lanes]
    for g in range(6, -1, -1):
        out = jnp.where(group == g, full[16 * g : 16 * g + 16, lanes], out)
    return out


def slab(ref, a, blk):
    return jnp.concatenate(
        [ref[16 * a : 16 * a + 144, blk], ref[16 * a + 16 : 16 * a + 160, blk]], axis=1
    )


def block_of(i):
    return pl.ds(pl.multiple_of(i * 128, 128), 128)


def lane_group():
    return lax.broadcasted_iota(jnp.int32, (16, 128), 1) // 16


def conv_block(i, q_ref, k_ref, v_ref, c_ref, u_ref, d_ref, b1_ref, b2_ref, outs):
    z_ref, gq_ref, gk_ref, gv_ref = outs
    blk = block_of(i)
    group = lane_group()
    lhs1 = b1_ref[blk, 0:144]
    lhs2 = b2_ref[blk, 0:144]
    for a in range(0, 8, 2):
        y = jnp.dot(lhs1, slab(u_ref, a, blk), preferred_element_type=F32)
        du = jnp.dot(lhs2, slab(d_ref, a, blk), preferred_element_type=F32)
        for half in range(2):
            rows = slice(16 * (a + half), 16 * (a + half) + 16)
            yv = pick(y, half, group)
            z_ref[rows, blk] = (q_ref[rows, blk].astype(F32) * yv).astype(BF16)
            gq_ref[rows, blk] = (c_ref[rows, blk].astype(F32) * yv).astype(BF16)
            dv = pick(du, half, group)
            gk_ref[rows, blk] = (v_ref[rows, blk].astype(F32) * dv).astype(BF16)
            gv_ref[rows, blk] = (k_ref[rows, blk].astype(F32) * dv).astype(BF16)


def pair_sums(i, u_ref, d_ref, g_ref):
    blk = block_of(i)
    group = lane_group()
    total = jnp.zeros((128, 144), F32)
    for a in range(0, 8, 2):
        pair = []
        for half in range(2):
            start = 128 + 16 * (a + half)
            rows = u_ref[start : start + 16, blk]
            spread = [jnp.where(group == g, rows, jnp.zeros_like(rows)) for g in range(8)]
            pair.append(jnp.concatenate(spread, axis=0))
        total = total + lax.dot_general(
            jnp.concatenate(pair, axis=1), slab(d_ref, a, blk), NT, preferred_element_type=F32
        )
    g_ref[blk, 0:144] = total


def diagonals(i, g_ref):
    rows = block_of(i)
    lane = lax.broadcasted_iota(jnp.int32, (128, 128), 1)
    r = lax.broadcasted_iota(jnp.int32, (128, 128), 0) % 16
    both = jnp.where(lane < r, g_ref[rows, 128:256], g_ref[rows, 0:128])
    parts = [
        both[16 * f : 16 * f + 8] + pltpu.roll(both[16 * f + 8 : 16 * f + 16], 120, 1)
        for f in range(8)
    ]
    sub = lax.broadcasted_iota(jnp.int32, (8, 128), 0)
    for step in (4, 2, 1):
        low = sub % (2 * step) < step
        merged = []
        for f in range(step):
            one, two = parts[f], parts[f + step]
            first = jnp.where(low, one, pltpu.roll(two, step, 0))
            second = jnp.where(low, pltpu.roll(one, 8 - step, 0), two)
            merged.append(first + pltpu.roll(second, 128 - step, 1))
        parts = merged
    return parts[0]


CHUNKS = 8
WIDE = 2048 // CHUNKS
SIZES = {"y": 4, "z": 8, "x": 4, "core": 2}
PLANE, LINE = ("y", "x", "core"), ("z",)


def place():
    ctx = lax.axis_index("ctx")
    return {
        "y": lax.axis_index("dp"),
        "z": ctx // 8,
        "x": lax.rem(ctx // 2, 4),
        "core": lax.rem(ctx, 2),
    }


def device(at):
    return {"dp": at["y"], "ctx": (at["z"] * 4 + at["x"]) * 2 + at["core"]}


def index_in(axes, at):
    index = 0
    for axis in axes:
        index = index * SIZES[axis] + at[axis]
    return index


def others(axes):
    def hops(offset):
        return sum(
            0.1 * d if axis == "core" else min(d, SIZES[axis] - d)
            for axis, d in zip(axes, offset)
        )

    every = itertools.product(*[range(SIZES[axis]) for axis in axes])
    return sorted([o for o in every if any(o)], key=lambda o: -hops(o))


def shifted(axes, at, offset):
    at = dict(at)
    for axis, d in zip(axes, offset):
        if d:
            at[axis] = lax.rem(at[axis] + d, SIZES[axis])
    return at


def beside(by):
    return {"ctx": lax.rem(lax.axis_index("ctx") + 64 + by, 64)}


def greet(at):
    barrier = pltpu.get_barrier_semaphore()
    count = 0
    for by in (1, -1):
        pl.semaphore_signal(barrier, 1, device_id=beside(by), device_id_type=MESH)
        count += 1
    for axes in (PLANE, LINE):
        for offset in others(axes):
            pl.semaphore_signal(
                barrier, 1, device_id=device(shifted(axes, at, offset)), device_id_type=MESH)
            count += 1
    return barrier, count


def send_all(axes, at, src_of, dst, send, recv):
    own = index_in(axes, at)
    for offset in others(axes):
        there = shifted(axes, at, offset)
        pltpu.make_async_remote_copy(
            src_of(index_in(axes, there)), dst.at[own], send, recv, device(there), MESH).start()


def wait_all(dst, sem):
    most = dst.at[pl.ds(0, dst.shape[0] - 1)]
    pltpu.make_async_copy(most, most, sem).wait()


def tree_sum(ref):
    terms = [ref[i] for i in range(ref.shape[0])]
    while len(terms) > 1:
        terms = [sum(terms[i : i + 2]) for i in range(0, len(terms), 2)]
    return terms[0]


def keep_of(starts_ref, position):
    hit = starts_ref[0, 0] == position
    for i in range(1, 17):
        hit = jnp.logical_or(hit, starts_ref[0, i] == position)
    return jnp.where(hit, 0.0, 1.0)


def whole_kernel(h_hbm, s_hbm, q_hbm, k_hbm, v_hbm, c_hbm,
                 z_ref, gq_ref, gk_ref, gv_ref, put_ref,
                 h_ref, s_ref, q_ref, k_ref, v_ref, c_ref,
                 u_ref, d_ref, us_ref, ds_ref, b1_ref, b2_ref, hs_ref, g_ref,
                 fg_ref, rs_buf, z_buf, part, loads,
                 u_send, u_recv, d_send, d_recv, sums):
    at = place()
    ctx = lax.axis_index("ctx")
    barrier, greeted = greet(at)
    pairs = ((h_hbm, h_ref), (s_hbm, s_ref), (k_hbm, k_ref), (v_hbm, v_ref), (q_hbm, q_ref), (c_hbm, c_ref))
    copies = [pltpu.make_async_copy(src, dst, loads.at[i]) for i, (src, dst) in enumerate(pairs)]
    for copy in copies:
        copy.start()
    for copy in copies[1:]:
        copy.wait()
    keep_own = keep_of(s_ref, ctx * 128)
    keep_after = keep_of(s_ref, (ctx + 1) * 128) * jnp.where(ctx == 63, 0.0, 1.0)

    def products(i, _):
        rows = pl.ds(pl.multiple_of(i * 16, 16), 16)
        below = pl.ds(pl.multiple_of(i * 16 + 128, 16), 16)
        u = k_ref[rows, :].astype(F32) * v_ref[rows, :].astype(F32)
        u_ref[below, :] = u.astype(BF16)
        us_ref[rows, :] = (u * keep_after).astype(BF16)
        dy = c_ref[rows, :].astype(F32) * q_ref[rows, :].astype(F32)
        d_ref[rows, :] = dy.astype(BF16)
        ds_ref[rows, :] = (dy * keep_own).astype(BF16)
        return 0

    lax.fori_loop(0, 8, products, 0)
    pl.semaphore_wait(barrier, greeted)

    def halo(j, by):
        lanes = pl.ds(pl.multiple_of(j * WIDE, WIDE), WIDE)
        if by == 1:
            return pltpu.make_async_remote_copy(
                us_ref.at[:, lanes], u_ref.at[pl.ds(0, 128), lanes],
                u_send.at[j], u_recv.at[j], beside(1), MESH)
        return pltpu.make_async_remote_copy(
            ds_ref.at[:, lanes], d_ref.at[pl.ds(128, 128), lanes],
            d_send.at[j], d_recv.at[j], beside(-1), MESH)

    def start(j, _):
        halo(j, -1).start()
        halo(j, 1).start()
        return 0

    lax.fori_loop(0, CHUNKS, start, 0)
    copies[0].wait()
    build_bases(h_ref, hs_ref, b1_ref, b2_ref)
    per = 16 // CHUNKS

    def sums_of(j):
        for i in range(per):
            pair_sums(j * per + i, u_ref, d_ref, g_ref)

    def diagonals_of(j):
        for i in range(per):
            rows = diagonals(j * per + i, g_ref)
            slot = 2 * (j * per + i)
            fg_ref[slot] = rows[0:4]
            fg_ref[slot + 1] = rows[4:8]

    halo(0, -1).wait_recv()
    sums_of(0)

    def arrive(j, _):
        halo(j, -1).wait_recv()
        diagonals_of(j - 1)
        sums_of(j)
        return 0

    lax.fori_loop(1, CHUNKS, arrive, 0)
    diagonals_of(CHUNKS - 1)

    own, height = index_in(PLANE, at), index_in(LINE, at)
    send_all(PLANE, at, lambda p: fg_ref.at[p], rs_buf, sums.at[0], sums.at[1])
    rs_buf[own] = fg_ref[own]

    def late(j, _):
        halo(j, 1).wait_recv()
        return 0

    lax.fori_loop(0, CHUNKS, late, 0)
    outs = (z_ref, gq_ref, gk_ref, gv_ref)

    def convolve(i, _):
        conv_block(i, q_ref, k_ref, v_ref, c_ref, u_ref, d_ref, b1_ref, b2_ref, outs)
        return 0

    lax.fori_loop(0, 12, convolve, 0)
    wait_all(rs_buf, sums.at[1])
    part[0] = tree_sum(rs_buf)
    send_all(LINE, at, lambda p: part.at[0], z_buf, sums.at[2], sums.at[3])
    z_buf[height] = part[0]
    lax.fori_loop(12, 16, convolve, 0)
    wait_all(z_buf, sums.at[3])
    part[1] = tree_sum(z_buf)
    send_all(PLANE, at, lambda p: part.at[1], put_ref, sums.at[4], sums.at[5])
    put_ref[own] = part[1]

    def sent(j, _):
        halo(j, -1).wait_send()
        halo(j, 1).wait_send()
        return 0

    lax.fori_loop(0, CHUNKS, sent, 0)
    wait_all(rs_buf, sums.at[0])
    wait_all(z_buf, sums.at[2])
    wait_all(put_ref, sums.at[4])
    wait_all(put_ref, sums.at[5])


def whole(h, starts, q, k, v, c):
    sd = jax.ShapeDtypeStruct
    vmem = pl.BlockSpec(memory_space=pltpu.VMEM)
    hbm = pl.BlockSpec(memory_space=pl.ANY)
    act = pltpu.VMEM((128, 2048), BF16)
    two = pltpu.VMEM((256, 2048), BF16)
    base = pltpu.VMEM((2048, 256), BF16)
    dma = pltpu.SemaphoreType.DMA
    return pl.pallas_call(
        whole_kernel,
        out_shape=[pltpu.VMEM((128, 2048), BF16)] * 4 + [pltpu.VMEM((32, 4, 128), F32)],
        in_specs=[hbm] * 6,
        out_specs=[vmem] * 5,
        scratch_shapes=[
            pltpu.VMEM((128, 128), BF16), pltpu.SMEM((1, 17), jnp.int32), act, act, act, act,
            two, two, act, act, base, base,
            pltpu.VMEM((2, 128, 128), F32), pltpu.VMEM((2048, 256), F32),
            pltpu.VMEM((32, 4, 128), F32), pltpu.VMEM((32, 4, 128), F32),
            pltpu.VMEM((8, 4, 128), F32), pltpu.VMEM((2, 4, 128), F32),
            dma((6,)), dma((CHUNKS,)), dma((CHUNKS,)), dma((CHUNKS,)), dma((CHUNKS,)), dma((6,)),
        ],
        compiler_params=pltpu.CompilerParams(
            collective_id=0, has_side_effects=True, vmem_limit_bytes=VMEM_LIMIT),
        name="whole_operator",
    )(*[pltpu.with_memory_space_constraint(x, pltpu.HBM) for x in (h, starts, q, k, v, c)])


VMEM_LIMIT = 32 * 1024 * 1024


def finish_kernel(*refs):
    sems = refs[10]
    copies = [pltpu.make_async_copy(refs[i], refs[5 + i], sems.at[i]) for i in range(5)]
    for copy in copies:
        copy.start()
    for copy in copies:
        copy.wait()


def finish(arrays):
    hbm = pl.BlockSpec(memory_space=pl.ANY)
    return pl.pallas_call(
        finish_kernel,
        out_shape=[pltpu.HBM(a.shape, a.dtype) for a in arrays],
        in_specs=[hbm] * 5,
        out_specs=[hbm] * 5,
        scratch_shapes=[pltpu.SemaphoreType.DMA((5,))],
        compiler_params=pltpu.CompilerParams(vmem_limit_bytes=1024 * 1024),
        name="finish",
    )(*[pltpu.with_memory_space_constraint(a, pltpu.VMEM) for a in arrays])


def per_device(gate_in, key_in, value_in, cotangent, doc_starts, filters):
    z, gq, gk, gv, put = finish(whole(
        filters, doc_starts, gate_in[0], key_in[0], value_in[0], cotangent[0]))
    return z[None], gq[None], gk[None], gv[None], put.reshape(128, 128)


def solution(mesh):
    rows = P("dp", "ctx", None)
    return jax.shard_map(
        per_device,
        mesh=mesh,
        in_specs=(rows, rows, rows, rows, P("dp", None), P()),
        out_specs=(rows, rows, rows, rows, P()),
        check_vma=False,
    )
```

time: 60.1 us -> 36.1 us (0.60)
  waiting for transfers between devices: 8.28 us -> 0 us
  Pallas kernels: 41 us -> 35.3 us
  starting transfers between devices: 3.36 us -> 0 us
  local copies, waits for them, and re-layouts: 2.92 us -> 0 us
  other arithmetic: 2.24 us -> 0 us
  between operations: 2.02 us -> 0.64 us
    ppermute x2 -> x0, waiting for transfers between devices: 8.28 us -> none  [the longest x1 4.58 us: per_device(): up = lax.ppermute(u, 'ctx', [(i, (i + 1) % 64) for i in range(64)])]
    pallas_call x2, Pallas kernels: 41 us -> 35.3 us  [the longest x1 34 us: whole(): pl.pallas_call(whole_kernel, out_shape=[pltpu.VMEM((128, 2048), BF16)] *...]
    ppermute x2 -> x0, starting transfers between devices: 3.36 us -> none  [the longest x1 2.67 us: per_device(): up = lax.ppermute(u, 'ctx', [(i, (i + 1) % 64) for i in range(64)])]
    unnamed x11 -> x0, local copies, waits for them, and re-layouts: 2.92 us -> none
    mul x2 -> x0, other arithmetic: 1.61 us -> none  [the longest x1 1.45 us: per_device(): u = (k.astype(F32) * v.astype(F32)).astype(BF16) * keep_after]
    reduce_or x1 -> x0, other arithmetic: 0.64 us -> none  [keeps(): own = jnp.any(starts == ctx * 128)]
  transfers between devices with their start and end apart: 2 -> 0, of which waited for: 2 -> 0; matrix products, arithmetic and copies ran while one was open for 0% -> 0% of each run, Pallas kernels for 0% -> 0%
where the time goes in v2:
time: 36.1 us; the launch traced here: 36 us
  Pallas kernels  35.3 us (98%)
  between operations  0.64 us (2%)
    pallas_call x1, Pallas kernels, whole(): pl.pallas_call(whole_kernel, out_shape=[pltpu.VMEM((128, 2048), BF16)] *...  34 us
    pallas_call x1, Pallas kernels, finish(): pl.pallas_call(finish_kernel, out_shape=[pltpu.HBM(a.shape, a.dtype) for...  1.37 us

profile of v2, /device:TPU:1, one launch (start us, length us, event | category | flops | bytes accessed | tf_op | source)
XLA Modules:
  0.0 36.0 jit_solution(4591634881508609342)
XLA Ops:
  0.6 34.0 %whole_operator.1 = (bf16[128,2048]{1,0:T(8,128)(2,1)S(1)}, bf16[128,2048]{1,0:T(8,128)(2,1)S(1)}, bf16[128,2048]{1,0:T(8,128)(2,1)S(1)}, bf16[128,2048]{1,0:T(8,128)(2,1)S(1)}, f32[32,4,128]{2,1,0:T(4,128)S(1)}) custom-call(bf16[128,128]{1,0:T(8,128)(2,1)} %h_hbm.1, s32[1,17]{1,0:T(1,128)} %s_hbm.1, bf16[128,2048]{1,0:T(8,128)(2,1)} %bitcast.9, ...), custom_call_target="tpu_custom_call" | custom-call | tf_op jit(solution)/shard_map/whole_operator/pallas_call | solution.py:334
  34.6 1.4 %finish.1 = (bf16[128,2048]{1,0:T(8,128)(2,1)}, bf16[128,2048]{1,0:T(8,128)(2,1)}, bf16[128,2048]{1,0:T(8,128)(2,1)}, bf16[128,2048]{1,0:T(8,128)(2,1)}, f32[32,4,128]{2,1,0:T(4,128)}) custom-call(bf16[128,2048]{1,0:T(8,128)(2,1)S(1)} %get-tuple-element.15.refs_0_, bf16[128,2048]{1,0:T(8,128)(2,1)S(1)} %get-tuple-element.16.refs_1_, ...), custom_call_target="tpu_custom_call" | custom-call | tf_op jit(solution)/shard_map/finish/pallas_call | solution.py:367

commit v3 on v2

--- a/solution.py
+++ b/solution.py
@@ -61,47 +61,40 @@
     return lax.broadcasted_iota(jnp.int32, (16, 128), 1) // 16
 
 
-def conv_block(i, q_ref, k_ref, v_ref, c_ref, u_ref, d_ref, b1_ref, b2_ref, outs):
-    z_ref, gq_ref, gk_ref, gv_ref = outs
+def conv_block(i, bases, source, gates, results):
     blk = block_of(i)
     group = lane_group()
-    lhs1 = b1_ref[blk, 0:144]
-    lhs2 = b2_ref[blk, 0:144]
+    lhs = bases[blk, 0:144]
     for a in range(0, 8, 2):
-        y = jnp.dot(lhs1, slab(u_ref, a, blk), preferred_element_type=F32)
-        du = jnp.dot(lhs2, slab(d_ref, a, blk), preferred_element_type=F32)
+        full = jnp.dot(lhs, slab(source, a, blk), preferred_element_type=F32)
         for half in range(2):
             rows = slice(16 * (a + half), 16 * (a + half) + 16)
-            yv = pick(y, half, group)
-            z_ref[rows, blk] = (q_ref[rows, blk].astype(F32) * yv).astype(BF16)
-            gq_ref[rows, blk] = (c_ref[rows, blk].astype(F32) * yv).astype(BF16)
-            dv = pick(du, half, group)
-            gk_ref[rows, blk] = (v_ref[rows, blk].astype(F32) * dv).astype(BF16)
-            gv_ref[rows, blk] = (k_ref[rows, blk].astype(F32) * dv).astype(BF16)
-
-
-def pair_sums(i, u_ref, d_ref, g_ref):
+            value = pick(full, half, group)
+            for gate, result in zip(gates, results):
+                result[rows, blk] = (gate[rows, blk].astype(F32) * value).astype(BF16)
+
+
+def pair_sums(i, slot, rows_ref, first, slab_ref, g_ref):
     blk = block_of(i)
     group = lane_group()
     total = jnp.zeros((128, 144), F32)
     for a in range(0, 8, 2):
         pair = []
         for half in range(2):
-            start = 128 + 16 * (a + half)
-            rows = u_ref[start : start + 16, blk]
+            start = first + 16 * (a + half)
+            rows = rows_ref[start : start + 16, blk]
             spread = [jnp.where(group == g, rows, jnp.zeros_like(rows)) for g in range(8)]
             pair.append(jnp.concatenate(spread, axis=0))
         total = total + lax.dot_general(
-            jnp.concatenate(pair, axis=1), slab(d_ref, a, blk), NT, preferred_element_type=F32
+            jnp.concatenate(pair, axis=1), slab(slab_ref, a, blk), NT, preferred_element_type=F32
         )
-    g_ref[blk, 0:144] = total
-
-
-def diagonals(i, g_ref):
-    rows = block_of(i)
+    g_ref[slot, :, 0:144] = total
+
+
+def diagonals(slot, g_ref, shift):
     lane = lax.broadcasted_iota(jnp.int32, (128, 128), 1)
     r = lax.broadcasted_iota(jnp.int32, (128, 128), 0) % 16
-    both = jnp.where(lane < r, g_ref[rows, 128:256], g_ref[rows, 0:128])
+    both = jnp.where(lane < r + shift, g_ref[slot, :, 128:256], g_ref[slot, :, 0:128])
     parts = [
         both[16 * f : 16 * f + 8] + pltpu.roll(both[16 * f + 8 : 16 * f + 16], 120, 1)
         for f in range(8)
@@ -120,9 +113,10 @@
 
 
 CHUNKS = 8
+HALF = CHUNKS // 2
 WIDE = 2048 // CHUNKS
 SIZES = {"y": 4, "z": 8, "x": 4, "core": 2}
-PLANE, LINE = ("y", "x", "core"), ("z",)
+PLANE, LINE = ("y", "x"), ("z", "core")
 
 
 def place():
@@ -183,6 +177,18 @@
     return barrier, count
 
 
+def group_of(at, step):
+    return lax.rem(at["y"] + (2, 1, 3, 0)[step], 4)
+
+
+def chunk_of(at, step):
+    return group_of(at, step % HALF) + (HALF if step >= HALF else 0)
+
+
+def block_at(y, x):
+    return 2 * y + x + jnp.where(x >= 2, 6, 0)
+
+
 def send_all(axes, at, src_of, dst, send, recv):
     own = index_in(axes, at)
     for offset in others(axes):
@@ -219,31 +225,49 @@
     at = place()
     ctx = lax.axis_index("ctx")
     barrier, greeted = greet(at)
-    pairs = ((h_hbm, h_ref), (s_hbm, s_ref), (k_hbm, k_ref), (v_hbm, v_ref), (q_hbm, q_ref), (c_hbm, c_ref))
-    copies = [pltpu.make_async_copy(src, dst, loads.at[i]) for i, (src, dst) in enumerate(pairs)]
-    for copy in copies:
-        copy.start()
-    for copy in copies[1:]:
-        copy.wait()
+    small = [
+        pltpu.make_async_copy(s_hbm, s_ref, loads.at[0]),
+        pltpu.make_async_copy(h_hbm, h_ref, loads.at[1]),
+    ]
+
+    def lanes_of(j):
+        return pl.ds(pl.multiple_of(j * WIDE, WIDE), WIDE)
+
+    def load(n, j):
+        src, dst = ((q_hbm, q_ref), (c_hbm, c_ref), (k_hbm, k_ref), (v_hbm, v_ref))[n]
+        return pltpu.make_async_copy(
+            src.at[:, lanes_of(j)], dst.at[:, lanes_of(j)], loads.at[2 + n * CHUNKS + j])
+
+    small[0].start()
+    for step in range(CHUNKS):
+        dy_chunk = chunk_of(at, step)
+        u_chunk = chunk_of(at, (step + HALF) % CHUNKS)
+        for n, j in ((0, dy_chunk), (1, dy_chunk), (2, u_chunk), (3, u_chunk)):
+            load(n, j).start()
+        if step == 0:
+            small[1].start()
+    small[0].wait()
     keep_own = keep_of(s_ref, ctx * 128)
     keep_after = keep_of(s_ref, (ctx + 1) * 128) * jnp.where(ctx == 63, 0.0, 1.0)
 
-    def products(i, _):
-        rows = pl.ds(pl.multiple_of(i * 16, 16), 16)
-        below = pl.ds(pl.multiple_of(i * 16 + 128, 16), 16)
-        u = k_ref[rows, :].astype(F32) * v_ref[rows, :].astype(F32)
-        u_ref[below, :] = u.astype(BF16)
-        us_ref[rows, :] = (u * keep_after).astype(BF16)
-        dy = c_ref[rows, :].astype(F32) * q_ref[rows, :].astype(F32)
-        d_ref[rows, :] = dy.astype(BF16)
-        ds_ref[rows, :] = (dy * keep_own).astype(BF16)
-        return 0
-
-    lax.fori_loop(0, 8, products, 0)
-    pl.semaphore_wait(barrier, greeted)
+    def dy_product(j):
+        load(0, j).wait()
+        load(1, j).wait()
+        lanes = lanes_of(j)
+        dy = c_ref[:, lanes].astype(F32) * q_ref[:, lanes].astype(F32)
+        d_ref[0:128, lanes] = dy.astype(BF16)
+        ds_ref[:, lanes] = (dy * keep_own).astype(BF16)
+
+    def u_product(j):
+        load(2, j).wait()
+        load(3, j).wait()
+        lanes = lanes_of(j)
+        u = k_ref[:, lanes].astype(F32) * v_ref[:, lanes].astype(F32)
+        u_ref[128:256, lanes] = u.astype(BF16)
+        us_ref[:, lanes] = (u * keep_after).astype(BF16)
 
     def halo(j, by):
-        lanes = pl.ds(pl.multiple_of(j * WIDE, WIDE), WIDE)
+        lanes = lanes_of(j)
         if by == 1:
             return pltpu.make_async_remote_copy(
                 us_ref.at[:, lanes], u_ref.at[pl.ds(0, 128), lanes],
@@ -252,64 +276,110 @@
             ds_ref.at[:, lanes], d_ref.at[pl.ds(128, 128), lanes],
             d_send.at[j], d_recv.at[j], beside(-1), MESH)
 
-    def start(j, _):
-        halo(j, -1).start()
-        halo(j, 1).start()
+    for step in range(HALF):
+        dy_chunk, u_chunk = chunk_of(at, step), chunk_of(at, step + HALF)
+        dy_product(dy_chunk)
+        u_product(u_chunk)
+        if step == 0:
+            pl.semaphore_wait(barrier, greeted)
+        halo(dy_chunk, -1).start()
+        halo(u_chunk, 1).start()
+    for step in range(HALF):
+        dy_product(chunk_of(at, step + HALF))
+        u_product(chunk_of(at, step))
+    small[1].wait()
+    build_bases(h_ref, hs_ref, b1_ref, b2_ref)
+    lane = lax.broadcasted_iota(jnp.int32, (128, 128), 1)
+    sub = lax.broadcasted_iota(jnp.int32, (128, 128), 0)
+    turn = jnp.where(lane + sub == 128, 1.0, jnp.where(lane + sub == 0, 1.0, 0.0))
+    per = 8 // HALF
+
+    def sums_of(step, j):
+        for i in range(per):
+            slot = 2 * (per * step + i)
+            pair_sums(j * per + i, slot, u_ref, 128, d_ref, g_ref)
+            pair_sums(8 + j * per + i, slot + 1, d_ref, 0, u_ref, g_ref)
+
+    def diagonals_of(step, j):
+        back = []
+        for i in range(per):
+            slot = 2 * (per * step + i)
+            fg_ref[j * per + i] = diagonals(slot, g_ref, 0)
+            back.append(diagonals(slot + 1, g_ref, 1))
+        back = jnp.dot(
+            jnp.concatenate(back, axis=0), turn,
+            precision=lax.Precision.HIGHEST, preferred_element_type=F32)
+        for i in range(per):
+            fg_ref[8 + j * per + i] = back[8 * i : 8 * i + 8]
+
+    own = at["y"] * 4 + at["x"]
+    mine = block_at(at["y"], at["x"])
+    height = index_in(LINE, at)
+
+    def hand_over(j, last):
+        for dx in (2, 1, 3) if last else (2, 1, 3, 0):
+            x = lax.rem(at["x"] + dx, 4)
+            there = device({"y": j, "z": at["z"], "x": x, "core": at["core"]})
+            pltpu.make_async_remote_copy(
+                fg_ref.at[block_at(j, x)], rs_buf.at[own], sums.at[0], sums.at[1], there, MESH
+            ).start()
+
+    before = None
+    for step in range(HALF):
+        j = group_of(at, step)
+        halo(j, -1).wait_recv()
+        halo(j + HALF, 1).wait_recv()
+        if before is not None:
+            diagonals_of(step - 1, before)
+        sums_of(step, j)
+        if before is not None:
+            hand_over(before, False)
+        before = j
+    diagonals_of(HALF - 1, before)
+    hand_over(before, True)
+    rs_buf[own] = fg_ref[mine]
+    for step in range(HALF):
+        halo(chunk_of(at, step + HALF), -1).start()
+        halo(chunk_of(at, step), 1).start()
+
+    def outputs(i):
+        conv_block(i, b1_ref, u_ref, (q_ref, c_ref), (z_ref, gq_ref))
+
+    def gradients(i):
+        conv_block(i, b2_ref, d_ref, (v_ref, k_ref), (gk_ref, gv_ref))
+
+    def early(i, _):
+        outputs(8 + i)
+        gradients(i)
         return 0
 
-    lax.fori_loop(0, CHUNKS, start, 0)
-    copies[0].wait()
-    build_bases(h_ref, hs_ref, b1_ref, b2_ref)
-    per = 16 // CHUNKS
-
-    def sums_of(j):
-        for i in range(per):
-            pair_sums(j * per + i, u_ref, d_ref, g_ref)
-
-    def diagonals_of(j):
-        for i in range(per):
-            rows = diagonals(j * per + i, g_ref)
-            slot = 2 * (j * per + i)
-            fg_ref[slot] = rows[0:4]
-            fg_ref[slot + 1] = rows[4:8]
-
-    halo(0, -1).wait_recv()
-    sums_of(0)
-
-    def arrive(j, _):
-        halo(j, -1).wait_recv()
-        diagonals_of(j - 1)
-        sums_of(j)
+    def later(i, _):
+        outputs(i)
+        gradients(8 + i)
         return 0
 
-    lax.fori_loop(1, CHUNKS, arrive, 0)
-    diagonals_of(CHUNKS - 1)
-
-    own, height = index_in(PLANE, at), index_in(LINE, at)
-    send_all(PLANE, at, lambda p: fg_ref.at[p], rs_buf, sums.at[0], sums.at[1])
-    rs_buf[own] = fg_ref[own]
-
-    def late(j, _):
-        halo(j, 1).wait_recv()
-        return 0
-
-    lax.fori_loop(0, CHUNKS, late, 0)
-    outs = (z_ref, gq_ref, gk_ref, gv_ref)
-
-    def convolve(i, _):
-        conv_block(i, q_ref, k_ref, v_ref, c_ref, u_ref, d_ref, b1_ref, b2_ref, outs)
-        return 0
-
-    lax.fori_loop(0, 12, convolve, 0)
+    lax.fori_loop(0, SPLIT[0], early, 0)
     wait_all(rs_buf, sums.at[1])
     part[0] = tree_sum(rs_buf)
     send_all(LINE, at, lambda p: part.at[0], z_buf, sums.at[2], sums.at[3])
     z_buf[height] = part[0]
-    lax.fori_loop(12, 16, convolve, 0)
+    lax.fori_loop(SPLIT[0], 8, early, 0)
+
+    def last_halo(j, _):
+        halo(j + HALF, -1).wait_recv()
+        halo(j, 1).wait_recv()
+        return 0
+
+    lax.fori_loop(0, HALF, last_halo, 0)
+    lax.fori_loop(0, SPLIT[1], later, 0)
     wait_all(z_buf, sums.at[3])
     part[1] = tree_sum(z_buf)
-    send_all(PLANE, at, lambda p: part.at[1], put_ref, sums.at[4], sums.at[5])
-    put_ref[own] = part[1]
+    for offset in others(PLANE):
+        there = device(shifted(PLANE, at, offset))
+        pltpu.make_async_remote_copy(
+            part.at[1], put_ref.at[mine], sums.at[4], sums.at[5], there, MESH).start()
+    put_ref[mine] = part[1]
+    lax.fori_loop(SPLIT[1], 8, later, 0)
 
     def sent(j, _):
         halo(j, -1).wait_send()
@@ -321,6 +391,9 @@
     wait_all(z_buf, sums.at[2])
     wait_all(put_ref, sums.at[4])
     wait_all(put_ref, sums.at[5])
+
+
+SPLIT = (6, 6)
 
 
 def whole(h, starts, q, k, v, c):
@@ -333,16 +406,16 @@
     dma = pltpu.SemaphoreType.DMA
     return pl.pallas_call(
         whole_kernel,
-        out_shape=[pltpu.VMEM((128, 2048), BF16)] * 4 + [pltpu.VMEM((32, 4, 128), F32)],
+        out_shape=[pltpu.VMEM((128, 2048), BF16)] * 4 + [pltpu.VMEM((16, 8, 128), F32)],
         in_specs=[hbm] * 6,
         out_specs=[vmem] * 5,
         scratch_shapes=[
             pltpu.VMEM((128, 128), BF16), pltpu.SMEM((1, 17), jnp.int32), act, act, act, act,
             two, two, act, act, base, base,
-            pltpu.VMEM((2, 128, 128), F32), pltpu.VMEM((2048, 256), F32),
-            pltpu.VMEM((32, 4, 128), F32), pltpu.VMEM((32, 4, 128), F32),
-            pltpu.VMEM((8, 4, 128), F32), pltpu.VMEM((2, 4, 128), F32),
-            dma((6,)), dma((CHUNKS,)), dma((CHUNKS,)), dma((CHUNKS,)), dma((CHUNKS,)), dma((6,)),
+            pltpu.VMEM((2, 128, 128), F32), pltpu.VMEM((16, 128, 256), F32),
+            pltpu.VMEM((16, 8, 128), F32), pltpu.VMEM((16, 8, 128), F32),
+            pltpu.VMEM((16, 8, 128), F32), pltpu.VMEM((2, 8, 128), F32),
+            dma((2 + 4 * CHUNKS,)), dma((CHUNKS,)), dma((CHUNKS,)), dma((CHUNKS,)), dma((CHUNKS,)), dma((6,)),
         ],
         compiler_params=pltpu.CompilerParams(
             collective_id=0, has_side_effects=True, vmem_limit_bytes=VMEM_LIMIT),

time: 36.1 us -> 34.8 us (0.964)
  Pallas kernels: 35.3 us -> 34.1 us
    pallas_call x1, Pallas kernels: 34 us -> 32.7 us  [whole(): pl.pallas_call(whole_kernel, out_shape=[pltpu.VMEM((128, 2048), BF16)] *...]
where the time goes in v3:
time: 34.8 us; the launch traced here: 34.7 us
  Pallas kernels  34.1 us (98%)
  between operations  0.64 us (2%)
    pallas_call x1, Pallas kernels, whole(): pl.pallas_call(whole_kernel, out_shape=[pltpu.VMEM((128, 2048), BF16)] *...  32.7 us
    pallas_call x1, Pallas kernels, finish(): pl.pallas_call(finish_kernel, out_shape=[pltpu.HBM(a.shape, a.dtype) for...  1.37 us

profile of v3, /device:TPU:1, one launch (start us, length us, event | category | flops | bytes accessed | tf_op | source)
XLA Modules:
  0.0 34.7 jit_solution(4154273998428533378)
XLA Ops:
  0.6 32.7 %whole_operator.1 = (bf16[128,2048]{1,0:T(8,128)(2,1)S(1)}, bf16[128,2048]{1,0:T(8,128)(2,1)S(1)}, bf16[128,2048]{1,0:T(8,128)(2,1)S(1)}, bf16[128,2048]{1,0:T(8,128)(2,1)S(1)}, f32[16,8,128]{2,1,0:T(8,128)S(1)}) custom-call(bf16[128,128]{1,0:T(8,128)(2,1)} %h_hbm.1, s32[1,17]{1,0:T(1,128)} %s_hbm.1, bf16[128,2048]{1,0:T(8,128)(2,1)} %bitcast.9, ...), custom_call_target="tpu_custom_call" | custom-call | tf_op jit(solution)/shard_map/whole_operator/pallas_call | solution.py:407
  33.3 1.4 %finish.1 = (bf16[128,2048]{1,0:T(8,128)(2,1)}, bf16[128,2048]{1,0:T(8,128)(2,1)}, bf16[128,2048]{1,0:T(8,128)(2,1)}, bf16[128,2048]{1,0:T(8,128)(2,1)}, f32[16,8,128]{2,1,0:T(8,128)}) custom-call(bf16[128,2048]{1,0:T(8,128)(2,1)S(1)} %get-tuple-element.15.refs_0_, bf16[128,2048]{1,0:T(8,128)(2,1)S(1)} %get-tuple-element.16.refs_1_, ...), custom_call_target="tpu_custom_call" | custom-call | tf_op jit(solution)/shard_map/finish/pallas_call | solution.py:440

commit v4 on v3

--- a/solution.py
+++ b/solution.py
@@ -112,9 +112,7 @@
     return parts[0]
 
 
-CHUNKS = 8
-HALF = CHUNKS // 2
-WIDE = 2048 // CHUNKS
+STEPS = ((0, 0, 2), (1, 0, 2), (2, 0, 2), (3, 0, 1), (3, 1, 1))
 SIZES = {"y": 4, "z": 8, "x": 4, "core": 2}
 PLANE, LINE = ("y", "x"), ("z", "core")
 
@@ -163,26 +161,50 @@
     return {"ctx": lax.rem(lax.axis_index("ctx") + 64 + by, 64)}
 
 
+NEAR = (("x", 1), ("x", 3), ("y", 1), ("y", 3), ("z", 1), ("z", 7), ("core", 1))
+
+
+def only(by, act):
+    ctx = lax.axis_index("ctx")
+    pl.when(ctx < 63 if by == 1 else ctx > 0)(act)
+
+
 def greet(at):
     barrier = pltpu.get_barrier_semaphore()
-    count = 0
     for by in (1, -1):
-        pl.semaphore_signal(barrier, 1, device_id=beside(by), device_id_type=MESH)
-        count += 1
-    for axes in (PLANE, LINE):
-        for offset in others(axes):
-            pl.semaphore_signal(
-                barrier, 1, device_id=device(shifted(axes, at, offset)), device_id_type=MESH)
-            count += 1
-    return barrier, count
+        only(by, lambda: pl.semaphore_signal(
+            barrier, 1, device_id=beside(by), device_id_type=MESH))
+    for axis, by in NEAR:
+        there = device(shifted((axis,), at, (by,)))
+        pl.semaphore_signal(barrier, 1, device_id=there, device_id_type=MESH)
+    ctx = lax.axis_index("ctx")
+    at_end = jnp.logical_or(ctx == 0, ctx == 63)
+    return barrier, jnp.where(at_end, 1, 2) + len(NEAR)
+
+
+ROUNDS = (
+    (("x", 3),),
+    (("y", 1), ("y", 3)),
+    (("y", 3),),
+    (("z", 1), ("z", 7)),
+    (("z", 1), ("z", 7)),
+    (("z", 1), ("z", 7)),
+    (("z", 7),),
+)
+
+
+def pass_on(at, known, n):
+    for axis, by in ROUNDS[n]:
+        there = device(shifted((axis,), at, (by,)))
+        pl.semaphore_signal(known.at[n], 1, device_id=there, device_id_type=MESH)
+
+
+def learn(known, n):
+    pl.semaphore_wait(known.at[n], len(ROUNDS[n]))
 
 
 def group_of(at, step):
     return lax.rem(at["y"] + (2, 1, 3, 0)[step], 4)
-
-
-def chunk_of(at, step):
-    return group_of(at, step % HALF) + (HALF if step >= HALF else 0)
 
 
 def block_at(y, x):
@@ -221,126 +243,158 @@
                  h_ref, s_ref, q_ref, k_ref, v_ref, c_ref,
                  u_ref, d_ref, us_ref, ds_ref, b1_ref, b2_ref, hs_ref, g_ref,
                  fg_ref, rs_buf, z_buf, part, loads,
-                 u_send, u_recv, d_send, d_recv, sums):
+                 u_send, u_recv, d_send, d_recv, sums, known):
     at = place()
     ctx = lax.axis_index("ctx")
+    halves = pl.ds(0, 1024), pl.ds(1024, 1024)
+    sides = ((q_hbm, q_ref), (c_hbm, c_ref)), ((k_hbm, k_ref), (v_hbm, v_ref))
+
+    def load(side, half):
+        return [
+            pltpu.make_async_copy(
+                src.at[:, halves[half]], dst.at[:, halves[half]], loads.at[4 * side + 2 * half + n])
+            for n, (src, dst) in enumerate(sides[side])
+        ]
+
+    small = [
+        pltpu.make_async_copy(s_hbm, s_ref, loads.at[8]),
+        pltpu.make_async_copy(h_hbm, h_ref, loads.at[9]),
+    ]
+    first = [small[0]] + load(0, 0) + load(1, 1)
+    for copy in first:
+        copy.start()
     barrier, greeted = greet(at)
-    small = [
-        pltpu.make_async_copy(s_hbm, s_ref, loads.at[0]),
-        pltpu.make_async_copy(h_hbm, h_ref, loads.at[1]),
-    ]
-
-    def lanes_of(j):
-        return pl.ds(pl.multiple_of(j * WIDE, WIDE), WIDE)
-
-    def load(n, j):
-        src, dst = ((q_hbm, q_ref), (c_hbm, c_ref), (k_hbm, k_ref), (v_hbm, v_ref))[n]
-        return pltpu.make_async_copy(
-            src.at[:, lanes_of(j)], dst.at[:, lanes_of(j)], loads.at[2 + n * CHUNKS + j])
-
-    small[0].start()
-    for step in range(CHUNKS):
-        dy_chunk = chunk_of(at, step)
-        u_chunk = chunk_of(at, (step + HALF) % CHUNKS)
-        for n, j in ((0, dy_chunk), (1, dy_chunk), (2, u_chunk), (3, u_chunk)):
-            load(n, j).start()
-        if step == 0:
-            small[1].start()
-    small[0].wait()
+    second = [small[1]] + load(0, 1) + load(1, 0)
+    for copy in second:
+        copy.start()
+    for copy in first:
+        copy.wait()
     keep_own = keep_of(s_ref, ctx * 128)
-    keep_after = keep_of(s_ref, (ctx + 1) * 128) * jnp.where(ctx == 63, 0.0, 1.0)
-
-    def dy_product(j):
-        load(0, j).wait()
-        load(1, j).wait()
-        lanes = lanes_of(j)
+    keep_after = keep_of(s_ref, (ctx + 1) * 128)
+
+    def dy_product(lanes):
         dy = c_ref[:, lanes].astype(F32) * q_ref[:, lanes].astype(F32)
         d_ref[0:128, lanes] = dy.astype(BF16)
         ds_ref[:, lanes] = (dy * keep_own).astype(BF16)
 
-    def u_product(j):
-        load(2, j).wait()
-        load(3, j).wait()
-        lanes = lanes_of(j)
+    def u_product(lanes):
         u = k_ref[:, lanes].astype(F32) * v_ref[:, lanes].astype(F32)
         u_ref[128:256, lanes] = u.astype(BF16)
         us_ref[:, lanes] = (u * keep_after).astype(BF16)
 
-    def halo(j, by):
-        lanes = lanes_of(j)
+    def halo(by, lanes, n):
         if by == 1:
             return pltpu.make_async_remote_copy(
                 us_ref.at[:, lanes], u_ref.at[pl.ds(0, 128), lanes],
-                u_send.at[j], u_recv.at[j], beside(1), MESH)
+                u_send.at[n], u_recv.at[n], beside(1), MESH)
         return pltpu.make_async_remote_copy(
             ds_ref.at[:, lanes], d_ref.at[pl.ds(128, 128), lanes],
-            d_send.at[j], d_recv.at[j], beside(-1), MESH)
-
-    for step in range(HALF):
-        dy_chunk, u_chunk = chunk_of(at, step), chunk_of(at, step + HALF)
-        dy_product(dy_chunk)
-        u_product(u_chunk)
+            d_send.at[n], d_recv.at[n], beside(-1), MESH)
+
+    def lanes_of(step, half):
+        quarter, skip, count = STEPS[step]
+        start = group_of(at, quarter) * 256 + 128 * skip + 1024 * half
+        return pl.ds(pl.multiple_of(start, 128), 128 * count)
+
+    def send(pair):
+        only(-1, pair[0].start)
+        only(1, pair[1].start)
+
+    def receive(pair):
+        only(1, pair[0].wait_recv)
+        only(-1, pair[1].wait_recv)
+
+    @pl.when(ctx == 0)
+    def _():
+        u_ref[0:128] = jnp.zeros((128, 2048), BF16)
+
+    @pl.when(ctx == 63)
+    def _():
+        d_ref[128:256] = jnp.zeros((128, 2048), BF16)
+
+    count = len(STEPS)
+    soon = [
+        (halo(-1, lanes_of(step, 0), step), halo(1, lanes_of(step, 1), step))
+        for step in range(count)
+    ]
+    rest = halo(-1, halves[1], count), halo(1, halves[0], count)
+    for step in range(count):
+        dy_product(lanes_of(step, 0))
+        u_product(lanes_of(step, 1))
         if step == 0:
             pl.semaphore_wait(barrier, greeted)
-        halo(dy_chunk, -1).start()
-        halo(u_chunk, 1).start()
-    for step in range(HALF):
-        dy_product(chunk_of(at, step + HALF))
-        u_product(chunk_of(at, step))
-    small[1].wait()
+        send(soon[step])
+        if step == 0:
+            pass_on(at, known, 0)
+            pass_on(at, known, 3)
+    for copy in second:
+        copy.wait()
+    for j in range(4):
+        dy_product(pl.ds(1024 + 256 * j, 256))
+        u_product(pl.ds(256 * j, 256))
+    learn(known, 0)
+    pass_on(at, known, 1)
+    learn(known, 3)
+    pass_on(at, known, 4)
     build_bases(h_ref, hs_ref, b1_ref, b2_ref)
+    learn(known, 1)
+    pass_on(at, known, 2)
+    learn(known, 4)
+    pass_on(at, known, 5)
     lane = lax.broadcasted_iota(jnp.int32, (128, 128), 1)
     sub = lax.broadcasted_iota(jnp.int32, (128, 128), 0)
     turn = jnp.where(lane + sub == 128, 1.0, jnp.where(lane + sub == 0, 1.0, 0.0))
-    per = 8 // HALF
-
-    def sums_of(step, j):
-        for i in range(per):
-            slot = 2 * (per * step + i)
-            pair_sums(j * per + i, slot, u_ref, 128, d_ref, g_ref)
-            pair_sums(8 + j * per + i, slot + 1, d_ref, 0, u_ref, g_ref)
-
-    def diagonals_of(step, j):
+
+    def blocks_of(step):
+        quarter, skip, blocks = STEPS[step]
+        start = group_of(at, quarter) * 2 + skip
+        slot = 4 * quarter + 2 * skip
+        return [(start + i, slot + 2 * i) for i in range(blocks)]
+
+    def sums_of(step):
+        for block, slot in blocks_of(step):
+            pair_sums(block, slot, u_ref, 128, d_ref, g_ref)
+            pair_sums(8 + block, slot + 1, d_ref, 0, u_ref, g_ref)
+
+    def diagonals_of(step):
         back = []
-        for i in range(per):
-            slot = 2 * (per * step + i)
-            fg_ref[j * per + i] = diagonals(slot, g_ref, 0)
+        for block, slot in blocks_of(step):
+            fg_ref[block] = diagonals(slot, g_ref, 0)
             back.append(diagonals(slot + 1, g_ref, 1))
         back = jnp.dot(
             jnp.concatenate(back, axis=0), turn,
             precision=lax.Precision.HIGHEST, preferred_element_type=F32)
-        for i in range(per):
-            fg_ref[8 + j * per + i] = back[8 * i : 8 * i + 8]
+        for i, (block, _) in enumerate(blocks_of(step)):
+            fg_ref[8 + block] = back[8 * i : 8 * i + 8]
 
     own = at["y"] * 4 + at["x"]
     mine = block_at(at["y"], at["x"])
     height = index_in(LINE, at)
 
-    def hand_over(j, last):
-        for dx in (2, 1, 3) if last else (2, 1, 3, 0):
+    def hand_over(quarter):
+        j = group_of(at, quarter)
+        for dx in (2, 1, 3) if quarter == 3 else (2, 1, 3, 0):
             x = lax.rem(at["x"] + dx, 4)
             there = device({"y": j, "z": at["z"], "x": x, "core": at["core"]})
             pltpu.make_async_remote_copy(
                 fg_ref.at[block_at(j, x)], rs_buf.at[own], sums.at[0], sums.at[1], there, MESH
             ).start()
 
-    before = None
-    for step in range(HALF):
-        j = group_of(at, step)
-        halo(j, -1).wait_recv()
-        halo(j + HALF, 1).wait_recv()
-        if before is not None:
-            diagonals_of(step - 1, before)
-        sums_of(step, j)
-        if before is not None:
-            hand_over(before, False)
-        before = j
-    diagonals_of(HALF - 1, before)
-    hand_over(before, True)
+    for step in range(count):
+        receive(soon[step])
+        if step > 0:
+            diagonals_of(step - 1)
+        sums_of(step)
+        if step == 1:
+            learn(known, 2)
+            learn(known, 5)
+            pass_on(at, known, 6)
+        if 0 < step < 4:
+            hand_over(step - 1)
+    diagonals_of(count - 1)
+    hand_over(3)
     rs_buf[own] = fg_ref[mine]
-    for step in range(HALF):
-        halo(chunk_of(at, step + HALF), -1).start()
-        halo(chunk_of(at, step), 1).start()
+    send(rest)
 
     def outputs(i):
         conv_block(i, b1_ref, u_ref, (q_ref, c_ref), (z_ref, gq_ref))
@@ -361,16 +415,12 @@
     lax.fori_loop(0, SPLIT[0], early, 0)
     wait_all(rs_buf, sums.at[1])
     part[0] = tree_sum(rs_buf)
+    learn(known, 6)
     send_all(LINE, at, lambda p: part.at[0], z_buf, sums.at[2], sums.at[3])
     z_buf[height] = part[0]
     lax.fori_loop(SPLIT[0], 8, early, 0)
 
-    def last_halo(j, _):
-        halo(j + HALF, -1).wait_recv()
-        halo(j, 1).wait_recv()
-        return 0
-
-    lax.fori_loop(0, HALF, last_halo, 0)
+    receive(rest)
     lax.fori_loop(0, SPLIT[1], later, 0)
     wait_all(z_buf, sums.at[3])
     part[1] = tree_sum(z_buf)
@@ -381,19 +431,16 @@
     put_ref[mine] = part[1]
     lax.fori_loop(SPLIT[1], 8, later, 0)
 
-    def sent(j, _):
-        halo(j, -1).wait_send()
-        halo(j, 1).wait_send()
-        return 0
-
-    lax.fori_loop(0, CHUNKS, sent, 0)
+    for pair in soon + [rest]:
+        only(-1, pair[0].wait_send)
+        only(1, pair[1].wait_send)
     wait_all(rs_buf, sums.at[0])
     wait_all(z_buf, sums.at[2])
     wait_all(put_ref, sums.at[4])
     wait_all(put_ref, sums.at[5])
 
 
-SPLIT = (6, 6)
+SPLIT = (3, 3)
 
 
 def whole(h, starts, q, k, v, c):
@@ -415,7 +462,8 @@
             pltpu.VMEM((2, 128, 128), F32), pltpu.VMEM((16, 128, 256), F32),
             pltpu.VMEM((16, 8, 128), F32), pltpu.VMEM((16, 8, 128), F32),
             pltpu.VMEM((16, 8, 128), F32), pltpu.VMEM((2, 8, 128), F32),
-            dma((2 + 4 * CHUNKS,)), dma((CHUNKS,)), dma((CHUNKS,)), dma((CHUNKS,)), dma((CHUNKS,)), dma((6,)),
+            dma((10,)), dma((6,)), dma((6,)), dma((6,)), dma((6,)), dma((6,)),
+            pltpu.SemaphoreType.REGULAR((len(ROUNDS),)),
         ],
         compiler_params=pltpu.CompilerParams(
             collective_id=0, has_side_effects=True, vmem_limit_bytes=VMEM_LIMIT),

time: 34.8 us -> 33.9 us (0.974)
  Pallas kernels: 34.1 us -> 33.1 us
    pallas_call x1, Pallas kernels: 32.7 us -> 31.7 us  [whole(): pl.pallas_call(whole_kernel, out_shape=[pltpu.VMEM((128, 2048), BF16)] *...]
where the time goes in v4:
time: 33.9 us; the launch traced here: 33.7 us
  Pallas kernels  33.1 us (98%)
  between operations  0.64 us (2%)
    pallas_call x1, Pallas kernels, whole(): pl.pallas_call(whole_kernel, out_shape=[pltpu.VMEM((128, 2048), BF16)] *...  31.7 us
    pallas_call x1, Pallas kernels, finish(): pl.pallas_call(finish_kernel, out_shape=[pltpu.HBM(a.shape, a.dtype) for...  1.37 us

profile of v4, /device:TPU:1, one launch (start us, length us, event | category | flops | bytes accessed | tf_op | source)
XLA Modules:
  0.0 33.7 jit_solution(6460059068411986474)
XLA Ops:
  0.6 31.7 %whole_operator.1 = (bf16[128,2048]{1,0:T(8,128)(2,1)S(1)}, bf16[128,2048]{1,0:T(8,128)(2,1)S(1)}, bf16[128,2048]{1,0:T(8,128)(2,1)S(1)}, bf16[128,2048]{1,0:T(8,128)(2,1)S(1)}, f32[16,8,128]{2,1,0:T(8,128)S(1)}) custom-call(bf16[128,128]{1,0:T(8,128)(2,1)} %h_hbm.1, s32[1,17]{1,0:T(1,128)} %s_hbm.1, bf16[128,2048]{1,0:T(8,128)(2,1)} %bitcast.9, ...), custom_call_target="tpu_custom_call" | custom-call | tf_op jit(solution)/shard_map/whole_operator/pallas_call | solution.py:454
  32.4 1.4 %finish.1 = (bf16[128,2048]{1,0:T(8,128)(2,1)}, bf16[128,2048]{1,0:T(8,128)(2,1)}, bf16[128,2048]{1,0:T(8,128)(2,1)}, bf16[128,2048]{1,0:T(8,128)(2,1)}, f32[16,8,128]{2,1,0:T(8,128)}) custom-call(bf16[128,2048]{1,0:T(8,128)(2,1)S(1)} %get-tuple-element.15.refs_0_, bf16[128,2048]{1,0:T(8,128)(2,1)S(1)} %get-tuple-element.16.refs_1_, ...), custom_call_target="tpu_custom_call" | custom-call | tf_op jit(solution)/shard_map/finish/pallas_call | solution.py:488

commit v5 on v4

--- a/solution.py
+++ b/solution.py
@@ -341,10 +341,6 @@
     pass_on(at, known, 2)
     learn(known, 4)
     pass_on(at, known, 5)
-    lane = lax.broadcasted_iota(jnp.int32, (128, 128), 1)
-    sub = lax.broadcasted_iota(jnp.int32, (128, 128), 0)
-    turn = jnp.where(lane + sub == 128, 1.0, jnp.where(lane + sub == 0, 1.0, 0.0))
-
     def blocks_of(step):
         quarter, skip, blocks = STEPS[step]
         start = group_of(at, quarter) * 2 + skip
@@ -357,15 +353,9 @@
             pair_sums(8 + block, slot + 1, d_ref, 0, u_ref, g_ref)
 
     def diagonals_of(step):
-        back = []
         for block, slot in blocks_of(step):
             fg_ref[block] = diagonals(slot, g_ref, 0)
-            back.append(diagonals(slot + 1, g_ref, 1))
-        back = jnp.dot(
-            jnp.concatenate(back, axis=0), turn,
-            precision=lax.Precision.HIGHEST, preferred_element_type=F32)
-        for i, (block, _) in enumerate(blocks_of(step)):
-            fg_ref[8 + block] = back[8 * i : 8 * i + 8]
+            fg_ref[8 + block] = diagonals(slot + 1, g_ref, 1)
 
     own = at["y"] * 4 + at["x"]
     mine = block_at(at["y"], at["x"])
@@ -475,11 +465,20 @@
 
 
 def finish_kernel(*refs):
-    sems = refs[10]
-    copies = [pltpu.make_async_copy(refs[i], refs[5 + i], sems.at[i]) for i in range(5)]
+    put_ref, put_hbm, sems, turned = refs[4], refs[9], refs[10], refs[11]
+    copies = [pltpu.make_async_copy(refs[i], refs[5 + i], sems.at[i]) for i in range(4)]
     for copy in copies:
         copy.start()
-    for copy in copies:
+    lane = lax.broadcasted_iota(jnp.int32, (128, 128), 1)
+    sub = lax.broadcasted_iota(jnp.int32, (128, 128), 0)
+    turn = jnp.where(lane + sub == 128, 1.0, jnp.where(lane + sub == 0, 1.0, 0.0))
+    turned[0:8] = put_ref[0:8]
+    turned[8:16] = jnp.dot(
+        put_ref[8:16].reshape(64, 128), turn,
+        precision=lax.Precision.HIGHEST, preferred_element_type=F32).reshape(8, 8, 128)
+    last = pltpu.make_async_copy(turned, put_hbm, sems.at[4])
+    last.start()
+    for copy in copies + [last]:
         copy.wait()
 
 
@@ -488,9 +487,9 @@
     return pl.pallas_call(
         finish_kernel,
         out_shape=[pltpu.HBM(a.shape, a.dtype) for a in arrays],
-        in_specs=[hbm] * 5,
+        in_specs=[hbm] * 4 + [pl.BlockSpec(memory_space=pltpu.VMEM)],
         out_specs=[hbm] * 5,
-        scratch_shapes=[pltpu.SemaphoreType.DMA((5,))],
+        scratch_shapes=[pltpu.SemaphoreType.DMA((5,)), pltpu.VMEM((16, 8, 128), F32)],
         compiler_params=pltpu.CompilerParams(vmem_limit_bytes=1024 * 1024),
         name="finish",
     )(*[pltpu.with_memory_space_constraint(a, pltpu.VMEM) for a in arrays])

time: 33.9 us -> 33.2 us (0.979)
  Pallas kernels: 33.1 us -> 32.4 us
    pallas_call x1, Pallas kernels: 31.7 us -> 31.1 us  [whole(): pl.pallas_call(whole_kernel, out_shape=[pltpu.VMEM((128, 2048), BF16)] *...]
where the time goes in v5:
time: 33.2 us; the launch traced here: 33.1 us
  Pallas kernels  32.4 us (98%)
  between operations  0.64 us (2%)
    pallas_call x1, Pallas kernels, whole(): pl.pallas_call(whole_kernel, out_shape=[pltpu.VMEM((128, 2048), BF16)] *...  31.1 us
    pallas_call x1, Pallas kernels, finish(): pl.pallas_call(finish_kernel, out_shape=[pltpu.HBM(a.shape, a.dtype) for...  1.37 us

profile of v5, /device:TPU:1, one launch (start us, length us, event | category | flops | bytes accessed | tf_op | source)
XLA Modules:
  0.0 33.1 jit_solution(15219348137678631231)
XLA Ops:
  0.6 31.1 %whole_operator.1 = (bf16[128,2048]{1,0:T(8,128)(2,1)S(1)}, bf16[128,2048]{1,0:T(8,128)(2,1)S(1)}, bf16[128,2048]{1,0:T(8,128)(2,1)S(1)}, bf16[128,2048]{1,0:T(8,128)(2,1)S(1)}, f32[16,8,128]{2,1,0:T(8,128)S(1)}) custom-call(bf16[128,128]{1,0:T(8,128)(2,1)} %h_hbm.1, s32[1,17]{1,0:T(1,128)} %s_hbm.1, bf16[128,2048]{1,0:T(8,128)(2,1)} %bitcast.9, ...), custom_call_target="tpu_custom_call" | custom-call | tf_op jit(solution)/shard_map/whole_operator/pallas_call | solution.py:444
  31.7 1.4 %finish.1 = (bf16[128,2048]{1,0:T(8,128)(2,1)}, bf16[128,2048]{1,0:T(8,128)(2,1)}, bf16[128,2048]{1,0:T(8,128)(2,1)}, bf16[128,2048]{1,0:T(8,128)(2,1)}, f32[16,8,128]{2,1,0:T(8,128)}) custom-call(bf16[128,2048]{1,0:T(8,128)(2,1)S(1)} %get-tuple-element.15.refs_0_, bf16[128,2048]{1,0:T(8,128)(2,1)S(1)} %get-tuple-element.16.refs_1_, ...), custom_call_target="tpu_custom_call" | custom-call | tf_op jit(solution)/shard_map/finish/pallas_call | solution.py:487
